TPU v7x, 256 devices: a whole 4x4x8 slice. The times are simulated.
256 devices in a mesh: tm: 64 (over y, z, core), space: 4 (over x).
Axes of the slice: x: 4, y: 4, z: 8, core: 2. Of those that a mesh axis runs over, the one named last changes fastest.
Arguments:
- snapshots: float32 [1024, 32, 2048], P('tm', None, 'space'), may hold values from -12 to 12
- quad_weights: float32 [2048], P('space'), may hold values from 0.25 to 4
Outputs:
- modes: float32 [2, 1024, 2048], P(None, 'tm', 'space')
- energies: float32 [1024], P('tm')
All inputs are finite; a program needn't handle non-finite values.
Results may differ from a plain program's by a relative error of at most 0.0001.
Values sent between devices are 32-bit elements; how exact they have to be, the bound alone decides.
A program may use at most 64 MiB of HBM per device.

v0:
```python
import math

import jax
import jax.numpy as jnp
from jax import lax
from jax.sharding import PartitionSpec as P

POWER = 3


def copy_for_each(array, axis):
    copies = jnp.broadcast_to(array, (lax.axis_size(axis), *array.shape))
    return lax.all_to_all(copies, axis, split_axis=0, concat_axis=0, tiled=True)


def of_everyone(array, axis):
    everything = copy_for_each(array, axis)
    return jnp.sum(everything, axis=0)


def packed_total(arrays, axis):
    ends = [0]
    for a in arrays:
        ends.append(ends[-1] + a.size)
    running = of_everyone(jnp.concatenate([a.ravel() for a in arrays]), axis)
    return tuple((running[b:e].reshape(a.shape) for a, b, e in zip(arrays, ends, ends[1:])))


def bit_reverse(values, bit_count):
    result = jnp.zeros_like(values)
    for position in range(bit_count):
        result = result + ((values >> position & 1) << bit_count - 1 - position)
    return result


def matvec(matrix, vector):
    return jnp.einsum("fbc,fc->fb", matrix, vector, precision=lax.Precision.HIGHEST)


def power_modes(real_gram, imag_gram):
    vec_real = jnp.ones(real_gram.shape[:2], jnp.float32) / math.sqrt(real_gram.shape[1])
    vec_imag = jnp.zeros(real_gram.shape[:2], jnp.float32)
    for sweep_idx in range(POWER):
        new_real = matvec(real_gram, vec_real) - matvec(imag_gram, vec_imag)
        new_imag = matvec(real_gram, vec_imag) + matvec(imag_gram, vec_real)
        length = lax.rsqrt(
            jnp.sum(new_real * new_real + new_imag * new_imag, axis=1, keepdims=True) + 1e-06
        )
        vec_real = new_real * length
        vec_imag = new_imag * length
    image_real = matvec(real_gram, vec_real) - matvec(imag_gram, vec_imag)
    image_imag = matvec(real_gram, vec_imag) + matvec(imag_gram, vec_real)
    energy = jnp.sum(vec_real * image_real + vec_imag * image_imag, axis=1)
    return (vec_real, vec_imag, energy)


def body(snapshots, quad_weights):
    tm_size = lax.axis_size("tm")
    bit_count = tm_size.bit_length() - 1
    local_times, blocks, points = snapshots.shape
    total_times = local_times * tm_size
    total_points = points * lax.axis_size("space")
    norm_factor = 1.0 / math.sqrt(0.375 * total_times)
    flattened = snapshots.reshape(local_times, blocks * points)
    columns = lax.all_to_all(flattened, "tm", split_axis=1, concat_axis=0, tiled=True)
    col_count = columns.shape[1]
    times_all = jnp.arange(total_times, dtype=jnp.int32)
    window = (
        0.5 - 0.5 * jnp.cos(2.0 * math.pi * times_all.astype(jnp.float32) / total_times)
    ) * norm_factor
    row_block = min(256, total_times)

    def one_block(block_idx):
        row_ids = block_idx * row_block + jnp.arange(row_block, dtype=jnp.int32)
        frequency = bit_reverse(row_ids // local_times, bit_count) + tm_size * (
            row_ids % local_times
        )
        angles = (
            -2.0
            * math.pi
            * (frequency[:, None] * times_all[None, :] % total_times).astype(jnp.float32)
            / total_times
        )
        cos_tab = jnp.cos(angles) * window[None, :]
        sin_tab = jnp.sin(angles) * window[None, :]
        return (
            jnp.dot(cos_tab, columns, precision=lax.Precision.HIGHEST),
            jnp.dot(sin_tab, columns, precision=lax.Precision.HIGHEST),
        )

    spec_real, spec_imag = lax.map(one_block, jnp.arange(total_times // row_block, dtype=jnp.int32))
    spectrum = jnp.stack(
        [spec_real.reshape(total_times, col_count), spec_imag.reshape(total_times, col_count)]
    )
    returned = lax.all_to_all(spectrum, "tm", split_axis=1, concat_axis=2, tiled=True)
    spectral = returned.reshape(2, local_times, blocks, points)
    weighted = spectral * quad_weights
    gram_full = (
        jnp.einsum("pfbx,qfcx->fpbqc", weighted, spectral, precision=lax.Precision.HIGHEST)
        / total_points
    )
    real_gram = gram_full[:, 0, :, 0] + gram_full[:, 1, :, 1]
    imag_gram = gram_full[:, 0, :, 1] - gram_full[:, 1, :, 0]
    real_gram, imag_gram = packed_total((real_gram, imag_gram), "space")
    vec_real, vec_imag, energy = power_modes(real_gram, imag_gram)
    inverse_root = lax.rsqrt(energy + 1e-06)[:, None]
    modes_real = jnp.einsum(
        "fb,fbx->fx", vec_real, spectral[0], precision=lax.Precision.HIGHEST
    ) - jnp.einsum("fb,fbx->fx", vec_imag, spectral[1], precision=lax.Precision.HIGHEST)
    modes_imag = jnp.einsum(
        "fb,fbx->fx", vec_imag, spectral[0], precision=lax.Precision.HIGHEST
    ) + jnp.einsum("fb,fbx->fx", vec_real, spectral[1], precision=lax.Precision.HIGHEST)
    return (jnp.stack([modes_real * inverse_root, modes_imag * inverse_root]), energy)


def solution(mesh):
    return jax.shard_map(
        body,
        mesh=mesh,
        in_specs=(P("tm", None, "space"), P("space")),
        out_specs=(P(None, "tm", "space"), P("tm")),
        check_vma=False,
    )
```

profile of v0, /device:TPU:1, one launch (start us, length us, event | category | flops | bytes accessed | tf_op | source)
XLA Modules:
  0.0 196.7 jit_solution(16553671760680132582)
XLA Ops:
  0.6 1.4 all_to_all.29
  2.0 1.6 copy.21
  3.6 13.1 %all-to-all-start = ((f32[16,64,256]{2,0,1:T(8,128)}), f32[16,64,256]{2,0,1:T(8,128)S(1)}, u32[]{:S(2)}, u32[]{:S(2)}) async-start(f32[16,64,256]{2,0,1:T(8,128)} %copy.21), calls=%async_computation | async-start | bytes 2097152 | tf_op jit(solution)/shard_map/all_to_all | solution.py:65
  16.8 28.5 %all-to-all-done = f32[16,64,256]{2,0,1:T(8,128)S(1)} async-done(((f32[16,64,256]{2,0,1:T(8,128)}), f32[16,64,256]{2,0,1:T(8,128)S(1)}, u32[]{:S(2)}, u32[]{:S(2)}) %all-to-all-start) | async-done | bytes 1048608 | tf_op jit(solution)/shard_map/all_to_all | solution.py:65
  45.3 45.3 %while.17 = (s32[]{:T(128)}, f32[4,256,256]{2,1,0:T(8,128)S(1)}, f32[4,256,256]{2,1,0:T(8,128)S(1)}, s32[4]{0:T(128)S(1)}, f32[1024,256]{1,0:T(8,128)S(1)}, /*index=5*/s32[]{:T(128)}, s32[1]{0:T(128)}) while((s32[]{:T(128)}, f32[4,256,256]{2,1,0:T(8,128)S(1)}, f32[4,256,256]{2,1,0:T(8,128)S(1)}, s32[4]{0:T(128)S(1)}, ...), condition=%wide.region_1.2_spmd.clone.clone, body=%wide.region_0.1_spmd.clone.clone.sunk | while | flops 1618493696 | bytes 2636913 | solution.py:91
  46.6 5.0 %fusion.120 = f32[4,256,256]{2,1,0:T(8,128)S(1)} fusion(f32[4,256,256]{2,1,0:T(8,128)S(1)} %get-tuple-element.235, s32[]{:T(128)} %get-tuple-element.234, f32[1024,256]{1,0:T(8,128)S(1)} %get-tuple-element.245, f32[1024]{0:T(1024)S(1)} %subtract_multiply_fusion.2, s32[256]{0:T(256)S(1)} %fusion.119), kind=kOutput, calls=%fused_computation.8.clone.1 | convolution fusion | flops 809238528 | bytes 1315844 | tf_op jit(solution)/shard_map/while/body/eval_jaxpr/dot_general | solution.py:87
  51.6 5.0 %fusion.121 = f32[4,256,256]{2,1,0:T(8,128)S(1)} fusion(f32[4,256,256]{2,1,0:T(8,128)S(1)} %get-tuple-element.236, s32[]{:T(128)} %get-tuple-element.234, f32[1024,256]{1,0:T(8,128)S(1)} %get-tuple-element.245, f32[1024]{0:T(1024)S(1)} %subtract_multiply_fusion.2, s32[256]{0:T(256)S(1)} %fusion.119), kind=kOutput, calls=%fused_computation.6.clone.1 | convolution fusion | flops 809238528 | bytes 1315844 | tf_op jit(solution)/shard_map/while/body/eval_jaxpr/dot_general | solution.py:88
  57.9 5.0 %fusion.120 = f32[4,256,256]{2,1,0:T(8,128)S(1)} fusion(f32[4,256,256]{2,1,0:T(8,128)S(1)} %get-tuple-element.235, s32[]{:T(128)} %get-tuple-element.234, f32[1024,256]{1,0:T(8,128)S(1)} %get-tuple-element.245, f32[1024]{0:T(1024)S(1)} %subtract_multiply_fusion.2, s32[256]{0:T(256)S(1)} %fusion.119), kind=kOutput, calls=%fused_computation.8.clone.1 | convolution fusion | flops 809238528 | bytes 1315844 | tf_op jit(solution)/shard_map/while/body/eval_jaxpr/dot_general | solution.py:87
  62.9 5.0 %fusion.121 = f32[4,256,256]{2,1,0:T(8,128)S(1)} fusion(f32[4,256,256]{2,1,0:T(8,128)S(1)} %get-tuple-element.236, s32[]{:T(128)} %get-tuple-element.234, f32[1024,256]{1,0:T(8,128)S(1)} %get-tuple-element.245, f32[1024]{0:T(1024)S(1)} %subtract_multiply_fusion.2, s32[256]{0:T(256)S(1)} %fusion.119), kind=kOutput, calls=%fused_computation.6.clone.1 | convolution fusion | flops 809238528 | bytes 1315844 | tf_op jit(solution)/shard_map/while/body/eval_jaxpr/dot_general | solution.py:88
  69.2 5.0 %fusion.120 = f32[4,256,256]{2,1,0:T(8,128)S(1)} fusion(f32[4,256,256]{2,1,0:T(8,128)S(1)} %get-tuple-element.235, s32[]{:T(128)} %get-tuple-element.234, f32[1024,256]{1,0:T(8,128)S(1)} %get-tuple-element.245, f32[1024]{0:T(1024)S(1)} %subtract_multiply_fusion.2, s32[256]{0:T(256)S(1)} %fusion.119), kind=kOutput, calls=%fused_computation.8.clone.1 | convolution fusion | flops 809238528 | bytes 1315844 | tf_op jit(solution)/shard_map/while/body/eval_jaxpr/dot_general | solution.py:87
  74.1 5.0 %fusion.121 = f32[4,256,256]{2,1,0:T(8,128)S(1)} fusion(f32[4,256,256]{2,1,0:T(8,128)S(1)} %get-tuple-element.236, s32[]{:T(128)} %get-tuple-element.234, f32[1024,256]{1,0:T(8,128)S(1)} %get-tuple-element.245, f32[1024]{0:T(1024)S(1)} %subtract_multiply_fusion.2, s32[256]{0:T(256)S(1)} %fusion.119), kind=kOutput, calls=%fused_computation.6.clone.1 | convolution fusion | flops 809238528 | bytes 1315844 | tf_op jit(solution)/shard_map/while/body/eval_jaxpr/dot_general | solution.py:88
  80.4 5.0 %fusion.120 = f32[4,256,256]{2,1,0:T(8,128)S(1)} fusion(f32[4,256,256]{2,1,0:T(8,128)S(1)} %get-tuple-element.235, s32[]{:T(128)} %get-tuple-element.234, f32[1024,256]{1,0:T(8,128)S(1)} %get-tuple-element.245, f32[1024]{0:T(1024)S(1)} %subtract_multiply_fusion.2, s32[256]{0:T(256)S(1)} %fusion.119), kind=kOutput, calls=%fused_computation.8.clone.1 | convolution fusion | flops 809238528 | bytes 1315844 | tf_op jit(solution)/shard_map/while/body/eval_jaxpr/dot_general | solution.py:87
  85.4 5.0 %fusion.121 = f32[4,256,256]{2,1,0:T(8,128)S(1)} fusion(f32[4,256,256]{2,1,0:T(8,128)S(1)} %get-tuple-element.236, s32[]{:T(128)} %get-tuple-element.234, f32[1024,256]{1,0:T(8,128)S(1)} %get-tuple-element.245, f32[1024]{0:T(1024)S(1)} %subtract_multiply_fusion.2, s32[256]{0:T(256)S(1)} %fusion.119), kind=kOutput, calls=%fused_computation.6.clone.1 | convolution fusion | flops 809238528 | bytes 1315844 | tf_op jit(solution)/shard_map/while/body/eval_jaxpr/dot_general | solution.py:88
  92.7 1.9 pad_maximum_fusion
  94.6 57.2 %all_to_all.40 = f32[2,1024,256]{2,0,1:T(2,128)S(1)} all-to-all(f32[2,1024,256]{2,0,1:T(2,128)S(1)} %pad_maximum_fusion), channel_id=1, replica_groups=mesh['tm'=64,'space'=4] {'tm'}, dimensions={1} | all-to-all | bytes 4194304 | tf_op jit(solution)/shard_map/all_to_all | solution.py:95
  152.0 2.6 %copy.23 = f32[2,16,64,256]{3,2,0,1:T(8,128)} copy(f32[2,16,64,256]{3,1,2,0:T(8,128)S(1)} %bitcast.171) | data formatting | bytes 4194304 | tf_op jit(solution)/shard_map/all_to_all | solution.py:95
  154.5 2.9 %reshape.128 = f32[2,16,32,512]{3,2,0,1:T(8,128)} reshape(f32[2,16,64,256]{3,2,0,1:T(8,128)} %copy.23) | data formatting | bytes 4194304 | tf_op jit(solution)/shard_map/reshape | solution.py:96
  157.4 2.9 %reshape.132 = f32[2,16,32,512,1]{3,2,0,1,4:T(8,128)} reshape(f32[2,16,64,256]{3,2,0,1:T(8,128)} %copy.23) | data formatting | bytes 4194304 | tf_op jit(solution)/shard_map/reshape | solution.py:96
  160.3 7.5 %fusion.34 = f32[16,2,32,2,32]{4,2,3,1,0:T(8,128)S(1)} fusion(f32[2,16,32,512,1]{3,2,0,1,4:T(8,128)} %reshape.132, f32[2,16,32,512]{3,2,0,1:T(8,128)} %reshape.128, f32[512]{0:T(512)S(1)} %copy-done), kind=kOutput, calls=%fused_computation.43 | convolution fusion | flops 403243008 | bytes 4458496 | tf_op jit(solution)/shard_map/pfbx,qfcx->fpbqc/dot_general | solution.py:99
  169.2 4.4 %all-to-all-start.2 = ((f32[4,1,32768]{2,1,0:T(1,128)}), f32[4,1,32768]{2,1,0:T(1,128)}, u32[]{:S(2)}, u32[]{:S(2)}) async-start(f32[4,1,32768]{2,1,0:T(1,128)} %broadcast_in_dim.30), calls=%async_computation.2 | async-start | bytes 1048576 | tf_op jit(solution)/shard_map/all_to_all | solution.py:13
  173.6 1.1 fusion.44
  175.7 1.8 copy.26
  177.8 4.7 %all-to-all-done.2 = f32[4,1,32768]{2,1,0:T(1,128)} async-done(((f32[4,1,32768]{2,1,0:T(1,128)}), f32[4,1,32768]{2,1,0:T(1,128)}, u32[]{:S(2)}, u32[]{:S(2)}) %all-to-all-start.2) | async-done | bytes 524320 | tf_op jit(solution)/shard_map/all_to_all | solution.py:13
  182.4 1.5 reduce_sum.45
  (68 shorter events, 20.1 us)
Async XLA Ops:
  3.6 41.7 %all-to-all-start = ((f32[16,64,256]{2,0,1:T(8,128)}), f32[16,64,256]{2,0,1:T(8,128)S(1)}, u32[]{:S(2)}, u32[]{:S(2)}) async-start(f32[16,64,256]{2,0,1:T(8,128)} %copy.21), calls=%async_computation | async-start | bytes 2097152 | tf_op jit(solution)/shard_map/all_to_all | solution.py:65
  157.4 2.9 %copy-start = (f32[512]{0:T(512)S(1)}, f32[512]{0:T(512)}, u32[]{:S(2)}) copy-start(f32[512]{0:T(512)} %param.5) | copy-start | bytes 6148
  169.2 13.2 %all-to-all-start.2 = ((f32[4,1,32768]{2,1,0:T(1,128)}), f32[4,1,32768]{2,1,0:T(1,128)}, u32[]{:S(2)}, u32[]{:S(2)}) async-start(f32[4,1,32768]{2,1,0:T(1,128)} %broadcast_in_dim.30), calls=%async_computation.2 | async-start | bytes 1048576 | tf_op jit(solution)/shard_map/all_to_all | solution.py:13
  196.0 0.7 copy-start.1
where the time goes:
time: 197 us
  matrix products  58.2 us (30%)
  blocking collectives  57.2 us (29%)
  waiting for transfers between devices  33.2 us (17%)
  local copies, waits for them, and re-layouts  21.6 us (11%)
  starting transfers between devices  17.5 us (9%)
  other arithmetic  5.21 us (3%)
  loops' own time  2.91 us (1%)
    all_to_all x1, blocking collectives, body(): lax.all_to_all(spectrum, 'tm', split_axis=1, concat_axis=2, tiled=True)  57.2 us
    all_to_all x1, waiting for transfers between devices, body(): lax.all_to_all(flattened, 'tm', split_axis=1, concat_axis=0, tiled=True)  28.5 us
    dot_general x4, matrix products, one_block(): jnp.dot(sin_tab, columns, precision=lax.Precision.HIGHEST)  19.9 us
    dot_general x4, matrix products, one_block(): jnp.dot(cos_tab, columns, precision=lax.Precision.HIGHEST)  19.8 us
    all_to_all x1, starting transfers between devices, body(): lax.all_to_all(flattened, 'tm', split_axis=1, concat_axis=0, tiled=True)  13.1 us
    dot_general x16, matrix products, matvec(): jnp.einsum('fbc,fc->fb', matrix, vector, precision=lax.Precision.HIGHEST)  8.46 us
    dot_general x1, matrix products, body(): jnp.einsum('pfbx,qfcx->fpbqc', weighted, spectral, precision=lax.Precisio...  7.54 us
    reshape x2, local copies, waits for them, and re-layouts, body(): spectral = returned.reshape(2, local_times, blocks, points)  5.73 us
  transfers between devices with their start and end apart: 2, of which 2 were waited for; matrix products, arithmetic and copies ran while one was open for 2% of the time, Pallas kernels for 0%

commit v1 on v0

v1 whole, which is shorter than its diff:
```python
import math

import jax
import jax.numpy as jnp
import numpy as np
from jax import lax
from jax.experimental import pallas as pl
from jax.experimental.pallas import tpu as pltpu
from jax.sharding import PartitionSpec as P

POWER = 3
F32 = jnp.float32
BF16 = jnp.bfloat16
MESH = pl.DeviceIdType.MESH
HIGHEST = lax.Precision.HIGHEST
NT = 1024
NX, NY, NZ, NC = 4, 4, 8, 2


def transform_table():
    t = np.arange(NT // 2)
    rows = []
    for unit in list(range(0, 32, 2)) + list(range(1, 32, 2)):
        if unit == 0:
            freq = np.array([64 * j for j in range(8)] + [32 + 64 * j for j in range(8)])
        else:
            freq = unit + 64 * np.arange(16)
        angle = 2.0 * np.pi * ((freq[:, None] * t[None, :]) % NT) / NT
        real, imag = np.cos(angle), -np.sin(angle)
        if unit == 0:
            imag[0] = np.cos(np.pi * t)
        rows += [real, imag]
    table = np.concatenate(rows).astype(np.float32)
    high = table.astype(jnp.bfloat16)
    low = (table - high.astype(np.float32)).astype(jnp.bfloat16)
    return np.stack([high, low])


def window_table():
    t = np.arange(NT)
    window = (0.5 - 0.5 * np.cos(2.0 * np.pi * t / NT)) / np.sqrt(0.375 * NT)
    return np.broadcast_to(window.astype(np.float32)[:, None], (NT, 128)).reshape(64, 16, 128)


def split(x):
    high = x.astype(BF16)
    return high, (x - high.astype(F32)).astype(BF16)


def dot(a, b):
    return jnp.dot(a, b, preferred_element_type=F32)


def dot_nt(a, b):
    return lax.dot_general(a, b, (((1,), (1,)), ((), ())), preferred_element_type=F32)


def interleave(first, second, low):
    crossed = pltpu.roll(jnp.where(low, second, first), 64, 1)
    return jnp.where(low, first, crossed), jnp.where(low, crossed, second)


def bit_reverse(value):
    result = 0
    for position in range(6):
        result = result + ((value >> position) & 1) * (1 << (5 - position))
    return result


def kernel(
    x_hbm, tab_hbm, win_hbm, w_ref, out_ref, e_ref,
    xin, win, tab, sb, rb, eh, ob, db, mh, ml, go, gr, vs, va, fs, fb,
    in_sem, tab_sem, s1, r1, s2, r2, s3, r3, s4, r4, s5, r5,
):
    me = lax.axis_index("tm")
    sx = lax.axis_index("space")
    y, z, c = me // 16, (me // 2) % 8, me % 2
    p = y * 2 + c
    yo = 3 - y
    unit = c * 16 + sx * 4 + (yo % 2) * 2 + yo // 2

    loads = [
        pltpu.make_async_copy(x_hbm.at[:, pl.ds(q * 128, 128)], xin.at[q], in_sem.at[q])
        for q in range(4)
    ]
    for load in loads:
        load.start()
    load_win = pltpu.make_async_copy(win_hbm.at[me], win, tab_sem.at[1])
    load_win.start()
    load_tab = pltpu.make_async_copy(tab_hbm, tab, tab_sem.at[0])
    load_tab.start()

    def unit_place(g):
        oy = (g % 2) * 2 + (g // 2) % 2
        return (g // 4) % 4, 3 - oy, g // 16

    barrier = pltpu.get_barrier_semaphore()

    @pl.loop(1, 64)
    def _(k):
        pl.semaphore_signal(barrier, 1, device_id=((me + k) % 64, sx), device_id_type=MESH)

    def peer(k):
        return (sx + k % 4) % 4, (y + k // 8) % 4, (c + (k // 4) % 2) % 2

    @pl.loop(1, 32)
    def _(k):
        px, py, pc = peer(k)
        pl.semaphore_signal(barrier, 1, device_id=(py * 16 + z * 2 + pc, px), device_id_type=MESH)

    mine = bit_reverse(me)
    my_unit = jnp.where(mine == 32, 0, jnp.where(mine > 32, 64 - mine, mine))
    ux, uy, uc = unit_place(my_unit)

    @pl.loop(0, 8)
    def _(k):
        pl.semaphore_signal(barrier, 1, device_id=(uy * 16 + k * 2 + uc, ux), device_id_type=MESH)

    lane = lax.broadcasted_iota(jnp.int32, (8, 128), 1)
    row = lax.broadcasted_iota(jnp.int32, (8, 128), 0)
    low = lane < 64
    root_w = jnp.sqrt(w_ref[...])
    load_win.wait()
    for load in loads:
        load.wait()
    factor = [
        [win[8 * sh : 8 * sh + 8, :] * root_w[:, 128 * q : 128 * q + 128] for q in range(4)]
        for sh in range(2)
    ]

    @pl.loop(0, 16)
    def _(bp):
        half, owner = bp % 2, bp // 2
        base = (owner // 2) * 16 + owner % 2
        for q in range(4):
            for sh in range(2):
                t0 = xin[q, pl.ds(sh * 256 + 2 * bp, 8, stride=32), :] * factor[sh][q]
                t1 = xin[q, pl.ds(sh * 256 + 2 * bp + 1, 8, stride=32), :] * factor[sh][q]
                even, odd = interleave(t0, t1, low)
                sb[half, base + 4 * q, 8 * sh : 8 * sh + 8, :] = even
                sb[half, base + 4 * q + 2, 8 * sh : 8 * sh + 8, :] = odd

    pl.semaphore_wait(barrier, 63 + 31 + 8)

    for h in range(2):

        @pl.loop(1, 64)
        def _(k):
            i = k % 8
            dz = jnp.where(i % 2 == 1, (i + 1) // 2, (8 - i // 2) % 8)
            py, pz, pc = (y + k // 16) % 4, (z + dz) % 8, (c + (k // 8) % 2) % 2
            to = py * 16 + pz * 2 + pc
            pltpu.make_async_remote_copy(
                sb.at[h, to], rb.at[h, me], s1.at[h], r1.at[h],
                device_id=(to, sx), device_id_type=MESH,
            ).start()

    for h in range(2):
        rb[h, me] = sb[h, me]

    load_tab.wait()
    for h in range(2):
        pltpu.make_async_copy(rb.at[h, pl.ds(0, 63)], rb.at[h, pl.ds(0, 63)], r1.at[h]).wait()

        @pl.loop(0, 8)
        def _(i):
            first = rb[h, pl.ds(i * 4, 4)].reshape(64, 128)
            second = rb[h, pl.ds(32 + i * 4, 4)].reshape(64, 128)
            for parity, value in enumerate((first + second, first - second)):
                high, rest = split(value)
                eh[parity, pl.ds(i * 64, 64), 0:128] = high
                eh[parity, pl.ds(i * 64, 64), 128:256] = rest

        @pl.loop(0, 8)
        def _(i):
            data = eh[i // 4]
            main = dot(tab[0, pl.ds(i * 128, 128), :], data)
            rest = dot(tab[1, pl.ds(i * 128, 128), :], data[:, 0:128])
            total = main[:, 0:128] + (main[:, 128:256] + rest)
            ob[h, pl.ds(i * 4, 4)] = total.reshape(4, 32, 128)

        here = pl.ds(pl.multiple_of((sx * 16 + 2 * p + h) * 32, 32), 32)

        @pl.loop(1, 32)
        def _(k):
            px, py, pc = peer(k)
            oy = 3 - py
            g = pc * 16 + px * 4 + (oy % 2) * 2 + oy // 2
            pltpu.make_async_remote_copy(
                ob.at[h, (g % 2) * 16 + g // 2], db.at[here], s2, r2,
                device_id=(py * 16 + z * 2 + pc, px), device_id_type=MESH,
            ).start()

        db[here, :] = ob[h, (unit % 2) * 16 + unit // 2]

    pltpu.make_async_copy(db.at[pl.ds(0, 62 * 32)], db.at[pl.ds(0, 62 * 32)], r2).wait()

    low16 = lax.broadcasted_iota(jnp.int32, (16, 128), 1) < 64

    @pl.loop(0, 8)
    def _(i):
        zt = (z + 1 + i) % 8
        grams = []
        for f in range(2):
            j = zt * 2 + f
            special = jnp.where((unit == 0) & (j == 0), 1.0, 0.0).astype(F32)
            planes = []
            for ri in range(2):
                tiles = []
                for q in range(2):
                    ta = db[pl.ds((2 * q) * 512 + ri * 16 + j, 16, stride=32), :]
                    tb = db[pl.ds((2 * q + 1) * 512 + ri * 16 + j, 16, stride=32), :]
                    tiles.append(jnp.concatenate(interleave(ta, tb, low16), axis=0))
                planes.append(jnp.concatenate(tiles, axis=1))
            real, imag = planes
            rh, rl = split(real)
            ih, il = split(imag)
            base = pl.multiple_of(j * 64, 64)
            mh[pl.ds(base, 32), :] = rh
            mh[pl.ds(base + 32, 32), :] = ih
            ml[pl.ds(base, 32), :] = rl
            ml[pl.ds(base + 32, 32), :] = il
            sh_, sl_ = split(imag * (1.0 - special))
            ch, cl = split(imag * special - real * (1.0 - special))
            left_h = jnp.concatenate([rh, ih], axis=1)
            left_l = jnp.concatenate([rl, il], axis=1)
            right_h = jnp.concatenate(
                [jnp.concatenate([rh, sh_], axis=1), jnp.concatenate([sh_, ch], axis=1)], axis=0
            )
            right_l = jnp.concatenate(
                [jnp.concatenate([rl, sl_], axis=1), jnp.concatenate([sl_, cl], axis=1)], axis=0
            )
            grams.append(
                dot_nt(left_h, right_h) + (dot_nt(left_h, right_l) + dot_nt(left_l, right_h))
            )
        pair = jnp.concatenate(grams, axis=1)

        @pl.when(i < 7)
        def _():
            go[zt] = pair
            pltpu.make_async_remote_copy(
                go.at[zt], gr.at[z], s3, r3,
                device_id=(y * 16 + zt * 2 + c, sx), device_id_type=MESH,
            ).start()

        @pl.when(i == 7)
        def _():
            gr[z] = pair

    pltpu.make_async_copy(gr.at[pl.ds(0, 7)], gr.at[pl.ds(0, 7)], r3).wait()
    gram = gr[0]
    for k in range(1, 8):
        gram = gram + gr[k]
    gram = gram * (1.0 / 2048.0)

    even = row % 2 == 0
    lone = (row < 2) & (unit == 0) & (z == 0)
    valid = (lane < 32) & (row < 4)

    def swap_rows(v):
        return jnp.where(even, pltpu.roll(v, 7, 0), pltpu.roll(v, 1, 0))

    def image_of(v):
        product = jnp.dot(v[:, 0:32], gram, preferred_element_type=F32, precision=HIGHEST)
        chosen = jnp.where(row < 2, product, pltpu.roll(product, 64, 1))
        other = pltpu.roll(chosen, 96, 1)
        crossed = swap_rows(other)
        normal = jnp.where(even, chosen + crossed, chosen - crossed)
        alone = jnp.where(even, chosen, other)
        return jnp.where(valid, jnp.where(lone, alone, normal), 0.0)

    def pair_sum(v):
        total = jnp.broadcast_to(jnp.sum(v, axis=1, keepdims=True), (8, 128))
        return jnp.where(lone, total, total + swap_rows(total))

    vec = jnp.where(valid & (even | lone), 1.0 / math.sqrt(32.0), 0.0).astype(F32)
    for _ in range(POWER):
        new = image_of(vec)
        vec = new * lax.rsqrt(pair_sum(new * new) + 1e-06)
    energy = pair_sum(vec * image_of(vec))
    scaled = vec * lax.rsqrt(energy + 1e-06)
    spread = scaled + pltpu.roll(scaled, 32, 1)
    spread = spread + pltpu.roll(spread, 64, 1)
    placed = lane // 32 == row
    vec_row = jnp.sum(jnp.where(placed, spread, 0.0), axis=0, keepdims=True)
    energy_row = jnp.sum(jnp.where(placed, energy, 0.0), axis=0, keepdims=True)
    message = jnp.where(row == 0, vec_row, jnp.where(row == 1, energy_row, 0.0))
    vs[...] = message
    va[z] = message

    @pl.loop(1, 8)
    def _(i):
        zt = (z + i) % 8
        pltpu.make_async_remote_copy(
            vs, va.at[z], s4, r4,
            device_id=(y * 16 + zt * 2 + c, sx), device_id_type=MESH,
        ).start()

    rows = lax.broadcasted_iota(jnp.int32, (64, 128), 0)
    lanes = lax.broadcasted_iota(jnp.int32, (64, 128), 1)
    ver, ri, j = rows // 32, (rows // 16) % 2, rows % 16
    first_unit = unit == 0
    slot = jnp.where(ver == 0, j, 15 - j)
    slot_first = jnp.where(
        ver == 0,
        jnp.where(j < 8, j, jnp.where(j == 8, 0, 16 - j)),
        jnp.where(j < 8, 8 + j, 23 - j),
    )
    slot = jnp.where(first_unit, slot_first, slot)
    mirrored = jnp.where(first_unit, j // 8, ver) == 1
    direct = first_unit & (ver == 0) & (j == 0)
    nyquist = first_unit & (ver == 0) & (j == 8)
    lane_imag = (lanes // 32) % 2 == 1
    lane_slot = lanes // 64
    straight = jnp.where(
        direct, jnp.where(lane_imag, 0.0, 1.0),
        jnp.where(nyquist, jnp.where(lane_imag, 1.0, 0.0), jnp.where(lane_imag, -1.0, 1.0)),
    )
    straight = jnp.where(ri == 0, straight, 0.0).astype(F32)
    across = jnp.where(direct | nyquist, 0.0, jnp.where(mirrored, -1.0, 1.0))
    across = jnp.where(ri == 0, 0.0, across).astype(F32)
    picked = lanes % 64 == jnp.where(nyquist, 32, 0)

    pltpu.make_async_copy(va.at[pl.ds(0, 7)], va.at[pl.ds(0, 7)], r4).wait()

    modes = jnp.zeros((64, 256), F32)
    energies = jnp.zeros((64, 128), F32)
    imag_row = (lax.broadcasted_iota(jnp.int32, (1, 128), 1) // 32) % 2 == 1
    for k in range(8):
        v = va[k, 0:1, :]
        e = va[k, 1:2, :]
        v_swapped = jnp.where(imag_row, pltpu.roll(v, 32, 1), pltpu.roll(v, 96, 1))
        here = slot == 2 * k + lane_slot
        left = jnp.where(here, straight * v + across * v_swapped, 0.0)
        energies = energies + jnp.where(here & picked, e, 0.0)
        lh, ll = split(left)
        high = mh[128 * k : 128 * k + 128, :]
        modes = modes + (dot(lh, high) + (dot(lh, ml[128 * k : 128 * k + 128, :]) + dot(ll, high)))
    energies = jnp.broadcast_to(jnp.sum(energies, axis=1, keepdims=True), (64, 128))

    sends = []
    for ver in range(2):
        if ver == 0:
            klass = unit
        else:
            klass = jnp.where(unit == 0, 32, 64 - unit)
        to = bit_reverse(klass)
        base = 32 * ver
        energy_tile = jnp.where(low, energies[base : base + 8], energies[base + 8 : base + 16])
        for px in range(4):
            n = ver * 4 + px
            q = 128 * (px // 2)
            for ri in range(2):
                a = modes[base + 16 * ri : base + 16 * ri + 8, q : q + 128]
                b = modes[base + 16 * ri + 8 : base + 16 * ri + 16, q : q + 128]
                if px % 2 == 0:
                    tile = jnp.where(low, a, pltpu.roll(b, 64, 1))
                else:
                    tile = jnp.where(low, pltpu.roll(a, 64, 1), b)
                fs[n, 8 * ri : 8 * ri + 8, :] = tile
            fs[n, 16:24, :] = energy_tile
            send = pltpu.make_async_remote_copy(
                fs.at[n], fb.at[z], s5.at[n], r5.at[z],
                device_id=(to, px), device_id_type=MESH,
            )
            send.start()
            sends.append(send)

    for k in range(8):
        pltpu.make_async_copy(fb.at[k], fb.at[k], r5.at[k]).wait()
    unscale = lax.rsqrt(w_ref[...])
    for q in range(4):
        for ri in range(2):
            a = fb[2 * q, 8 * ri : 8 * ri + 8, :]
            b = fb[2 * q + 1, 8 * ri : 8 * ri + 8, :]
            first, second = interleave(a, b, low)
            scale = unscale[:, 128 * q : 128 * q + 128]
            out_ref[16 * ri : 16 * ri + 8, 128 * q : 128 * q + 128] = first * scale
            out_ref[16 * ri + 8 : 16 * ri + 16, 128 * q : 128 * q + 128] = second * scale
    e_tile = fb[0, 16:24, :]
    e_ref[0:8, :] = e_tile
    e_ref[8:16, :] = pltpu.roll(e_tile, 64, 1)

    for h in range(2):
        pltpu.make_async_copy(sb.at[h, pl.ds(0, 63)], sb.at[h, pl.ds(0, 63)], s1.at[h]).wait()
    pltpu.make_async_copy(db.at[pl.ds(0, 62 * 32)], db.at[pl.ds(0, 62 * 32)], s2).wait()
    pltpu.make_async_copy(gr.at[pl.ds(0, 7)], gr.at[pl.ds(0, 7)], s3).wait()
    pltpu.make_async_copy(va.at[pl.ds(0, 7)], va.at[pl.ds(0, 7)], s4).wait()
    for send in sends:
        send.wait_send()


def body(snapshots, quad_weights):
    times, blocks, points = snapshots.shape
    table = jnp.asarray(transform_table())
    window = jnp.asarray(window_table())
    any_spec = pl.BlockSpec(memory_space=pl.ANY)
    vmem = pl.BlockSpec(memory_space=pltpu.VMEM)
    dma = pltpu.SemaphoreType.DMA
    modes, energies = pl.pallas_call(
        kernel,
        out_shape=(
            jax.ShapeDtypeStruct((32, 512), F32),
            jax.ShapeDtypeStruct((16, 128), F32),
        ),
        in_specs=[any_spec, any_spec, any_spec, vmem],
        out_specs=(vmem, vmem),
        scratch_shapes=[
            pltpu.VMEM((4, 512, 128), F32),
            pltpu.VMEM((16, 128), F32),
            pltpu.VMEM((2, 1024, 512), BF16),
            pltpu.VMEM((2, 64, 16, 128), F32),
            pltpu.VMEM((2, 64, 16, 128), F32),
            pltpu.VMEM((2, 512, 256), BF16),
            pltpu.VMEM((2, 32, 32, 128), F32),
            pltpu.VMEM((2048, 128), F32),
            pltpu.VMEM((1024, 256), BF16),
            pltpu.VMEM((1024, 256), BF16),
            pltpu.VMEM((8, 32, 128), F32),
            pltpu.VMEM((8, 32, 128), F32),
            pltpu.VMEM((8, 128), F32),
            pltpu.VMEM((8, 8, 128), F32),
            pltpu.VMEM((8, 24, 128), F32),
            pltpu.VMEM((8, 24, 128), F32),
            dma((4,)), dma((2,)),
            dma((2,)), dma((2,)),
            dma, dma, dma, dma, dma, dma,
            dma((8,)), dma((8,)),
        ],
        compiler_params=pltpu.CompilerParams(collective_id=0, has_side_effects=True),
        name="spod",
    )(
        snapshots.reshape(times * blocks, points), table, window, quad_weights.reshape(1, points)
    )
    return modes.reshape(2, 16, points), energies[:, 0]


def solution(mesh):
    return jax.shard_map(
        body,
        mesh=mesh,
        in_specs=(P("tm", None, "space"), P("space")),
        out_specs=(P(None, "tm", "space"), P("tm")),
        check_vma=False,
    )
```

time: 197 us -> 82.6 us (0.42)
  Pallas kernels: 0 us -> 77.2 us
  matrix products: 58.2 us -> 0 us
  blocking collectives: 57.2 us -> 0 us
  waiting for transfers between devices: 33.2 us -> 0 us
  starting transfers between devices: 17.5 us -> 0 us
  local copies, waits for them, and re-layouts: 21.6 us -> 4.55 us
  other arithmetic: 5.21 us -> 0 us
  loops' own time: 2.91 us -> 0 us
    pallas_call x0 -> x1, Pallas kernels: none -> 77.2 us  [body(): pl.pallas_call(kernel, out_shape=(jax.ShapeDtypeStruct((32, 512), F32), j...]
    dot_general x29 -> x0, matrix products: 58.2 us -> none  [the longest x4 19.9 us: one_block(): jnp.dot(sin_tab, columns, precision=lax.Precision.HIGHEST)]
    all_to_all x1 -> x0, blocking collectives: 57.2 us -> none  [body(): lax.all_to_all(spectrum, 'tm', split_axis=1, concat_axis=2, tiled=True)]
    all_to_all x2 -> x0, waiting for transfers between devices: 33.2 us -> none  [the longest x1 28.5 us: body(): lax.all_to_all(flattened, 'tm', split_axis=1, concat_axis=0, tiled=True)]
    all_to_all x2 -> x0, starting transfers between devices: 17.5 us -> none  [the longest x1 13.1 us: body(): lax.all_to_all(flattened, 'tm', split_axis=1, concat_axis=0, tiled=True)]
    reshape x4 -> x0, local copies, waits for them, and re-layouts: 5.96 us -> none  [the longest x2 5.73 us: body(): spectral = returned.reshape(2, local_times, blocks, points)]
    all_to_all x4 -> x0, local copies, waits for them, and re-layouts: 5.7 us -> none  [the longest x2 2.99 us: body(): lax.all_to_all(flattened, 'tm', split_axis=1, concat_axis=0, tiled=True)]
    another operation x1 -> x0, loops' own time: 2.91 us -> none  [body(): lax.map(one_block, jnp.arange(total_times // row_block, dtype=jnp.int32))]
  transfers between devices with their start and end apart: 2 -> 0, of which waited for: 2 -> 0; matrix products, arithmetic and copies ran while one was open for 2% -> 0% of each run, Pallas kernels for 0% -> 0%
where the time goes in v1:
time: 82.6 us; the launch traced here: 82.4 us
  Pallas kernels  77.2 us (93%)
  local copies, waits for them, and re-layouts  4.55 us (6%)
    pallas_call x1, Pallas kernels, body(): pl.pallas_call(kernel, out_shape=(jax.ShapeDtypeStruct((32, 512), F32), j...  77.2 us
    another operation x1, local copies, waits for them, and re-layouts  1.75 us

profile of v1, /device:TPU:1, one launch (start us, length us, event | category | flops | bytes accessed | tf_op | source)
XLA Modules:
  0.0 82.4 jit_solution(4692018170370716678)
XLA Ops:
  0.6 1.8 %jit_solution_.3.win_hbm = f32[64,16,128]{2,1,0:T(8,128)} broadcast(f32[64,16]{1,0:T(8,128)} %constant.5.clone), dimensions={0,1} | broadcast | bytes 528384 | tf_op jit(solution)
  2.4 77.2 %spod.1 = (f32[32,512]{1,0:T(8,128)}, f32[16,128]{1,0:T(8,128)}) custom-call(f32[512,512]{1,0:T(8,128)} %bitcast.3, bf16[2,1024,512]{2,1,0:T(8,128)(2,1)} %constant.4.clone.tab_hbm, f32[64,16,128]{2,1,0:T(8,128)} %jit_solution_.3.win_hbm, f32[1,512]{1,0:T(1,128)} %bitcast.5), custom_call_target="tpu_custom_call" | custom-call | tf_op jit(solution)/shard_map/spod/pallas_call | solution.py:400
  79.6 1.3 %slice_reduce_fusion = f32[16]{0:T(128)} fusion(f32[16,128]{1,0:T(8,128)} %get-tuple-element.5), kind=kLoop, calls=%fused_computation | loop fusion | bytes 128 | tf_op jit(solution)/shard_map/slice | solution.py:435
  80.9 1.5 %copy.7 = f32[2,16,512]{2,1,0:T(8,128)} copy(f32[2,16,512]{2,1,0:T(8,128)} %bitcast.4) | data formatting | bytes 131072

commit v2 on v1

--- a/solution.py
+++ b/solution.py
@@ -36,12 +36,6 @@
     return np.stack([high, low])
 
 
-def window_table():
-    t = np.arange(NT)
-    window = (0.5 - 0.5 * np.cos(2.0 * np.pi * t / NT)) / np.sqrt(0.375 * NT)
-    return np.broadcast_to(window.astype(np.float32)[:, None], (NT, 128)).reshape(64, 16, 128)
-
-
 def split(x):
     high = x.astype(BF16)
     return high, (x - high.astype(F32)).astype(BF16)
@@ -67,17 +61,24 @@
     return result
 
 
+def unit_of(x, y, c):
+    return c * 16 + x * 4 + ((y & 1) << 1) + (y >> 1)
+
+
+def far_first(z, i):
+    return (z + jnp.where((i & 1) == 1, 4 - ((i + 1) >> 1), 4 + (i >> 1))) & 7
+
+
 def kernel(
-    x_hbm, tab_hbm, win_hbm, w_ref, out_ref, e_ref,
-    xin, win, tab, sb, rb, eh, ob, db, mh, ml, go, gr, vs, va, fs, fb,
-    in_sem, tab_sem, s1, r1, s2, r2, s3, r3, s4, r4, s5, r5,
+    x_hbm, tab_hbm, w_ref, out_ref,
+    xin, tab, sb, rb, eh, ob, db, mh, ml, go, gr, vs, va, fs, fb,
+    in_sem, tab_sem, row_sem, s1, r1, s2, r2, s3, r3, s4, r4, s5, r5,
 ):
     me = lax.axis_index("tm")
     sx = lax.axis_index("space")
-    y, z, c = me // 16, (me // 2) % 8, me % 2
+    y, z, c = me >> 4, (me >> 1) & 7, me & 1
     p = y * 2 + c
-    yo = 3 - y
-    unit = c * 16 + sx * 4 + (yo % 2) * 2 + yo // 2
+    unit = unit_of(sx, y, c)
 
     loads = [
         pltpu.make_async_copy(x_hbm.at[:, pl.ds(q * 128, 128)], xin.at[q], in_sem.at[q])
@@ -85,53 +86,46 @@
     ]
     for load in loads:
         load.start()
-    load_win = pltpu.make_async_copy(win_hbm.at[me], win, tab_sem.at[1])
-    load_win.start()
-    load_tab = pltpu.make_async_copy(tab_hbm, tab, tab_sem.at[0])
+    load_tab = pltpu.make_async_copy(tab_hbm, tab, tab_sem)
     load_tab.start()
 
-    def unit_place(g):
-        oy = (g % 2) * 2 + (g // 2) % 2
-        return (g // 4) % 4, 3 - oy, g // 16
-
     barrier = pltpu.get_barrier_semaphore()
 
-    @pl.loop(1, 64)
+    def greet(semaphore, tm, space):
+        pl.semaphore_signal(semaphore, 1, device_id=(tm, space), device_id_type=MESH)
+
+    @pl.loop(1, 16)
     def _(k):
-        pl.semaphore_signal(barrier, 1, device_id=((me + k) % 64, sx), device_id_type=MESH)
+        greet(barrier, (me & 48) + ((me + k) & 15), sx)
+
+    @pl.loop(1, 4)
+    def _(k):
+        greet(barrier, (me + 16 * k) & 63, sx)
+        greet(barrier, me, (sx + k) & 3)
 
     def peer(k):
-        return (sx + k % 4) % 4, (y + k // 8) % 4, (c + (k // 4) % 2) % 2
-
-    @pl.loop(1, 32)
-    def _(k):
-        px, py, pc = peer(k)
-        pl.semaphore_signal(barrier, 1, device_id=(py * 16 + z * 2 + pc, px), device_id_type=MESH)
-
-    mine = bit_reverse(me)
-    my_unit = jnp.where(mine == 32, 0, jnp.where(mine > 32, 64 - mine, mine))
-    ux, uy, uc = unit_place(my_unit)
-
-    @pl.loop(0, 8)
-    def _(k):
-        pl.semaphore_signal(barrier, 1, device_id=(uy * 16 + k * 2 + uc, ux), device_id_type=MESH)
+        return (sx + k) & 3, (y + (k >> 3)) & 3, c ^ ((k >> 2) & 1)
 
     lane = lax.broadcasted_iota(jnp.int32, (8, 128), 1)
     row = lax.broadcasted_iota(jnp.int32, (8, 128), 0)
     low = lane < 64
     root_w = jnp.sqrt(w_ref[...])
-    load_win.wait()
     for load in loads:
         load.wait()
-    factor = [
-        [win[8 * sh : 8 * sh + 8, :] * root_w[:, 128 * q : 128 * q + 128] for q in range(4)]
-        for sh in range(2)
-    ]
+    factor = []
+    for sh in range(2):
+        phase = (row + (16 * me + 8 * sh - NT // 2)).astype(F32) * (math.pi / NT)
+        square = phase * phase
+        cosine = jnp.full((8, 128), 1.0 / math.factorial(16), F32)
+        for n in range(14, -1, -2):
+            cosine = cosine * square + (-1.0) ** (n // 2) / math.factorial(n)
+        window = cosine * cosine * (1.0 / math.sqrt(0.375 * NT))
+        factor.append([window * root_w[:, 128 * q : 128 * q + 128] for q in range(4)])
 
     @pl.loop(0, 16)
     def _(bp):
-        half, owner = bp % 2, bp // 2
-        base = (owner // 2) * 16 + owner % 2
+        half, owner = bp & 1, bp >> 1
+        base = (owner >> 1) * 16 + (owner & 1)
         for q in range(4):
             for sh in range(2):
                 t0 = xin[q, pl.ds(sh * 256 + 2 * bp, 8, stride=32), :] * factor[sh][q]
@@ -140,20 +134,26 @@
                 sb[half, base + 4 * q, 8 * sh : 8 * sh + 8, :] = even
                 sb[half, base + 4 * q + 2, 8 * sh : 8 * sh + 8, :] = odd
 
-    pl.semaphore_wait(barrier, 63 + 31 + 8)
-
-    for h in range(2):
-
-        @pl.loop(1, 64)
-        def _(k):
-            i = k % 8
-            dz = jnp.where(i % 2 == 1, (i + 1) // 2, (8 - i // 2) % 8)
-            py, pz, pc = (y + k // 16) % 4, (z + dz) % 8, (c + (k // 8) % 2) % 2
-            to = py * 16 + pz * 2 + pc
+    pl.semaphore_wait(barrier, 15 + 3 + 3)
+    for k in range(1, 4):
+        greet(row_sem, (me + 16 * k) & 63, sx)
+
+    def send_columns(h):
+        def send(k):
+            i = k & 7
+            dz = jnp.where((i & 1) == 1, (i + 1) >> 1, 8 - (i >> 1))
+            to = (((y + (k >> 4)) & 3) << 4) + (((z + dz) & 7) << 1) + (c ^ ((k >> 3) & 1))
             pltpu.make_async_remote_copy(
                 sb.at[h, to], rb.at[h, me], s1.at[h], r1.at[h],
                 device_id=(to, sx), device_id_type=MESH,
             ).start()
+
+        return send
+
+    pl.loop(1, 16)(send_columns(0))
+    pl.semaphore_wait(row_sem, 3)
+    pl.loop(16, 64)(send_columns(0))
+    pl.loop(1, 64)(send_columns(1))
 
     for h in range(2):
         rb[h, me] = sb[h, me]
@@ -173,7 +173,7 @@
 
         @pl.loop(0, 8)
         def _(i):
-            data = eh[i // 4]
+            data = eh[i >> 2]
             main = dot(tab[0, pl.ds(i * 128, 128), :], data)
             rest = dot(tab[1, pl.ds(i * 128, 128), :], data[:, 0:128])
             total = main[:, 0:128] + (main[:, 128:256] + rest)
@@ -184,14 +184,13 @@
         @pl.loop(1, 32)
         def _(k):
             px, py, pc = peer(k)
-            oy = 3 - py
-            g = pc * 16 + px * 4 + (oy % 2) * 2 + oy // 2
+            g = unit_of(px, py, pc)
             pltpu.make_async_remote_copy(
-                ob.at[h, (g % 2) * 16 + g // 2], db.at[here], s2, r2,
-                device_id=(py * 16 + z * 2 + pc, px), device_id_type=MESH,
+                ob.at[h, (g & 1) * 16 + (g >> 1)], db.at[here], s2, r2,
+                device_id=((py << 4) + (z << 1) + pc, px), device_id_type=MESH,
             ).start()
 
-        db[here, :] = ob[h, (unit % 2) * 16 + unit // 2]
+        db[here, :] = ob[h, (unit & 1) * 16 + (unit >> 1)]
 
     pltpu.make_async_copy(db.at[pl.ds(0, 62 * 32)], db.at[pl.ds(0, 62 * 32)], r2).wait()
 
@@ -199,7 +198,7 @@
 
     @pl.loop(0, 8)
     def _(i):
-        zt = (z + 1 + i) % 8
+        zt = far_first(z, i)
         grams = []
         for f in range(2):
             j = zt * 2 + f
@@ -240,7 +239,7 @@
             go[zt] = pair
             pltpu.make_async_remote_copy(
                 go.at[zt], gr.at[z], s3, r3,
-                device_id=(y * 16 + zt * 2 + c, sx), device_id_type=MESH,
+                device_id=((y << 4) + (zt << 1) + c, sx), device_id_type=MESH,
             ).start()
 
         @pl.when(i == 7)
@@ -288,12 +287,12 @@
     vs[...] = message
     va[z] = message
 
-    @pl.loop(1, 8)
+    @pl.loop(0, 7)
     def _(i):
-        zt = (z + i) % 8
+        zt = far_first(z, i)
         pltpu.make_async_remote_copy(
             vs, va.at[z], s4, r4,
-            device_id=(y * 16 + zt * 2 + c, sx), device_id_type=MESH,
+            device_id=((y << 4) + (zt << 1) + c, sx), device_id_type=MESH,
         ).start()
 
     rows = lax.broadcasted_iota(jnp.int32, (64, 128), 0)
@@ -363,11 +362,45 @@
                 fs.at[n], fb.at[z], s5.at[n], r5.at[z],
                 device_id=(to, px), device_id_type=MESH,
             )
-            send.start()
-            sends.append(send)
-
+            kept = (to == me) & (px == sx)
+            sends.append((send, kept))
+
+            @pl.when(jnp.logical_not(kept))
+            def _():
+                send.start()
+
+            @pl.when(kept)
+            def _():
+                fb[z] = fs[n]
+
+    mine = bit_reverse(me)
+    my_unit = jnp.where(mine == 32, 0, jnp.where(mine > 32, 64 - mine, mine))
+    same_group = my_unit == unit
     for k in range(8):
-        pltpu.make_async_copy(fb.at[k], fb.at[k], r5.at[k]).wait()
+
+        @pl.when(jnp.logical_not(same_group & (z == k)))
+        def _():
+            pltpu.make_async_copy(fb.at[k], fb.at[k], r5.at[k]).wait()
+
+    for k in range(8):
+        out_ref[k] = fb[k]
+
+    for h in range(2):
+        pltpu.make_async_copy(sb.at[h, pl.ds(0, 63)], sb.at[h, pl.ds(0, 63)], s1.at[h]).wait()
+    pltpu.make_async_copy(db.at[pl.ds(0, 62 * 32)], db.at[pl.ds(0, 62 * 32)], s2).wait()
+    pltpu.make_async_copy(gr.at[pl.ds(0, 7)], gr.at[pl.ds(0, 7)], s3).wait()
+    pltpu.make_async_copy(va.at[pl.ds(0, 7)], va.at[pl.ds(0, 7)], s4).wait()
+    for send, kept in sends:
+
+        @pl.when(jnp.logical_not(kept))
+        def _():
+            send.wait_send()
+
+
+def unpack(fb, w_ref, out_ref, e_ref):
+    lane = lax.broadcasted_iota(jnp.int32, (8, 128), 1)
+    row = lax.broadcasted_iota(jnp.int32, (8, 128), 0)
+    low = lane < 64
     unscale = lax.rsqrt(w_ref[...])
     for q in range(4):
         for ri in range(2):
@@ -377,37 +410,26 @@
             scale = unscale[:, 128 * q : 128 * q + 128]
             out_ref[16 * ri : 16 * ri + 8, 128 * q : 128 * q + 128] = first * scale
             out_ref[16 * ri + 8 : 16 * ri + 16, 128 * q : 128 * q + 128] = second * scale
-    e_tile = fb[0, 16:24, :]
-    e_ref[0:8, :] = e_tile
-    e_ref[8:16, :] = pltpu.roll(e_tile, 64, 1)
-
-    for h in range(2):
-        pltpu.make_async_copy(sb.at[h, pl.ds(0, 63)], sb.at[h, pl.ds(0, 63)], s1.at[h]).wait()
-    pltpu.make_async_copy(db.at[pl.ds(0, 62 * 32)], db.at[pl.ds(0, 62 * 32)], s2).wait()
-    pltpu.make_async_copy(gr.at[pl.ds(0, 7)], gr.at[pl.ds(0, 7)], s3).wait()
-    pltpu.make_async_copy(va.at[pl.ds(0, 7)], va.at[pl.ds(0, 7)], s4).wait()
-    for send in sends:
-        send.wait_send()
+    tile = fb[0, 16:24, :]
+    turned = pltpu.roll(tile, 64, 1)
+    diagonal = jnp.where(lane == row, tile, 0.0) + jnp.where(lane == row + 8, turned, 0.0)
+    e_ref[...] = jnp.sum(diagonal, axis=0, keepdims=True)[:, 0:16]
 
 
 def body(snapshots, quad_weights):
     times, blocks, points = snapshots.shape
     table = jnp.asarray(transform_table())
-    window = jnp.asarray(window_table())
     any_spec = pl.BlockSpec(memory_space=pl.ANY)
     vmem = pl.BlockSpec(memory_space=pltpu.VMEM)
     dma = pltpu.SemaphoreType.DMA
-    modes, energies = pl.pallas_call(
+    weights = quad_weights.reshape(1, points)
+    packed = pl.pallas_call(
         kernel,
-        out_shape=(
-            jax.ShapeDtypeStruct((32, 512), F32),
-            jax.ShapeDtypeStruct((16, 128), F32),
-        ),
-        in_specs=[any_spec, any_spec, any_spec, vmem],
-        out_specs=(vmem, vmem),
+        out_shape=jax.ShapeDtypeStruct((8, 24, 128), F32),
+        in_specs=[any_spec, any_spec, vmem],
+        out_specs=vmem,
         scratch_shapes=[
             pltpu.VMEM((4, 512, 128), F32),
-            pltpu.VMEM((16, 128), F32),
             pltpu.VMEM((2, 1024, 512), BF16),
             pltpu.VMEM((2, 64, 16, 128), F32),
             pltpu.VMEM((2, 64, 16, 128), F32),
@@ -422,17 +444,25 @@
             pltpu.VMEM((8, 8, 128), F32),
             pltpu.VMEM((8, 24, 128), F32),
             pltpu.VMEM((8, 24, 128), F32),
-            dma((4,)), dma((2,)),
+            dma((4,)), dma, pltpu.SemaphoreType.REGULAR,
             dma((2,)), dma((2,)),
             dma, dma, dma, dma, dma, dma,
             dma((8,)), dma((8,)),
         ],
         compiler_params=pltpu.CompilerParams(collective_id=0, has_side_effects=True),
         name="spod",
-    )(
-        snapshots.reshape(times * blocks, points), table, window, quad_weights.reshape(1, points)
-    )
-    return modes.reshape(2, 16, points), energies[:, 0]
+    )(snapshots.reshape(times * blocks, points), table, weights)
+    modes, energies = pl.pallas_call(
+        unpack,
+        out_shape=(
+            jax.ShapeDtypeStruct((32, points), F32),
+            jax.ShapeDtypeStruct((1, 16), F32),
+        ),
+        in_specs=[vmem, vmem],
+        out_specs=(vmem, vmem),
+        name="unpack",
+    )(packed, weights)
+    return modes.reshape(2, 16, points), energies.reshape(16)
 
 
 def solution(mesh):

time: 82.6 us -> 74.8 us (0.906)
  local copies, waits for them, and re-layouts: 4.55 us -> 0 us
  Pallas kernels: 77.2 us -> 74 us
    pallas_call x1 -> x2, Pallas kernels: 77.2 us -> 74 us  [the longest x1 72.4 us: body(): pl.pallas_call(kernel, out_shape=jax.ShapeDtypeStruct((8, 24, 128), F32),...]
    another operation x1 -> x0, local copies, waits for them, and re-layouts: 1.75 us -> none
    unnamed x1 -> x0, local copies, waits for them, and re-layouts: 1.47 us -> none
    slice x1 -> x0, local copies, waits for them, and re-layouts: 1.32 us -> none  [body(): return (modes.reshape(2, 16, points), energies[:, 0])]
where the time goes in v2:
time: 74.8 us; the launch traced here: 74.6 us
  Pallas kernels  74 us (99%)
    pallas_call x1, Pallas kernels, body(): pl.pallas_call(kernel, out_shape=jax.ShapeDtypeStruct((8, 24, 128), F32),...  72.4 us
    pallas_call x1, Pallas kernels, body(): pl.pallas_call(unpack, out_shape=(jax.ShapeDtypeStruct((32, points), F32)...  1.61 us

profile of v2, /device:TPU:1, one launch (start us, length us, event | category | flops | bytes accessed | tf_op | source)
XLA Modules:
  0.0 74.6 jit_solution(4965807556521732813)
XLA Ops:
  0.6 72.4 %spod.1.fb = f32[8,24,128]{2,1,0:T(8,128)} custom-call(f32[512,512]{1,0:T(8,128)} %bitcast.4, bf16[2,1024,512]{2,1,0:T(8,128)(2,1)} %constant.2.clone.tab_hbm, f32[1,512]{1,0:T(1,128)} %bitcast.5), custom_call_target="tpu_custom_call" | custom-call | tf_op jit(solution)/shard_map/spod/pallas_call | solution.py:426
  73.0 1.6 %unpack.1 = (f32[32,512]{1,0:T(8,128)}, f32[1,16]{1,0:T(1,128)}) custom-call(f32[8,24,128]{2,1,0:T(8,128)} %spod.1.fb, f32[1,512]{1,0:T(1,128)} %bitcast.6), custom_call_target="tpu_custom_call" | custom-call | tf_op jit(solution)/shard_map/unpack/pallas_call | solution.py:455

commit v3 on v2

--- a/solution.py
+++ b/solution.py
@@ -18,7 +18,7 @@
 
 
 def transform_table():
-    t = np.arange(NT // 2)
+    t = np.arange(NT // 2).reshape(32, 2, 8).transpose(1, 0, 2).reshape(-1)
     rows = []
     for unit in list(range(0, 32, 2)) + list(range(1, 32, 2)):
         if unit == 0:
@@ -122,17 +122,16 @@
         window = cosine * cosine * (1.0 / math.sqrt(0.375 * NT))
         factor.append([window * root_w[:, 128 * q : 128 * q + 128] for q in range(4)])
 
-    @pl.loop(0, 16)
-    def _(bp):
-        half, owner = bp & 1, bp >> 1
+    @pl.loop(0, 32)
+    def _(b):
+        owner = b >> 2
         base = (owner >> 1) * 16 + (owner & 1)
         for q in range(4):
-            for sh in range(2):
-                t0 = xin[q, pl.ds(sh * 256 + 2 * bp, 8, stride=32), :] * factor[sh][q]
-                t1 = xin[q, pl.ds(sh * 256 + 2 * bp + 1, 8, stride=32), :] * factor[sh][q]
-                even, odd = interleave(t0, t1, low)
-                sb[half, base + 4 * q, 8 * sh : 8 * sh + 8, :] = even
-                sb[half, base + 4 * q + 2, 8 * sh : 8 * sh + 8, :] = odd
+            t0 = xin[q, pl.ds(b, 8, stride=32), :] * factor[0][q]
+            t1 = xin[q, pl.ds(256 + b, 8, stride=32), :] * factor[1][q]
+            even, odd = interleave(t0, t1, low)
+            sb[b & 3, base + 4 * q] = even
+            sb[b & 3, base + 4 * q + 2] = odd
 
     pl.semaphore_wait(barrier, 15 + 3 + 3)
     for k in range(1, 4):
@@ -153,33 +152,40 @@
     pl.loop(1, 16)(send_columns(0))
     pl.semaphore_wait(row_sem, 3)
     pl.loop(16, 64)(send_columns(0))
-    pl.loop(1, 64)(send_columns(1))
-
-    for h in range(2):
+    for h in range(1, 4):
+        pl.loop(1, 64)(send_columns(h))
+
+    for h in range(4):
         rb[h, me] = sb[h, me]
 
     load_tab.wait()
-    for h in range(2):
+    low64 = lax.broadcasted_iota(jnp.int32, (64, 128), 1) < 64
+    low16 = lax.broadcasted_iota(jnp.int32, (16, 128), 1) < 64
+    for h in range(4):
         pltpu.make_async_copy(rb.at[h, pl.ds(0, 63)], rb.at[h, pl.ds(0, 63)], r1.at[h]).wait()
 
-        @pl.loop(0, 8)
+        @pl.loop(0, 4)
         def _(i):
-            first = rb[h, pl.ds(i * 4, 4)].reshape(64, 128)
-            second = rb[h, pl.ds(32 + i * 4, 4)].reshape(64, 128)
+            first = rb[h, pl.ds(i * 8, 8)].reshape(64, 128)
+            second = rb[h, pl.ds(32 + i * 8, 8)].reshape(64, 128)
             for parity, value in enumerate((first + second, first - second)):
-                high, rest = split(value)
-                eh[parity, pl.ds(i * 64, 64), 0:128] = high
-                eh[parity, pl.ds(i * 64, 64), 128:256] = rest
+                high = value.astype(BF16).astype(F32)
+                early, late = interleave(high, value - high, low64)
+                eh[parity, pl.ds(i * 64, 64), :] = early.astype(BF16)
+                eh[parity, pl.ds(256 + i * 64, 64), :] = late.astype(BF16)
 
         @pl.loop(0, 8)
         def _(i):
             data = eh[i >> 2]
-            main = dot(tab[0, pl.ds(i * 128, 128), :], data)
-            rest = dot(tab[1, pl.ds(i * 128, 128), :], data[:, 0:128])
-            total = main[:, 0:128] + (main[:, 128:256] + rest)
-            ob[h, pl.ds(i * 4, 4)] = total.reshape(4, 32, 128)
-
-        here = pl.ds(pl.multiple_of((sx * 16 + 2 * p + h) * 32, 32), 32)
+            total = dot(tab[0, pl.ds(i * 128, 128), :], data)
+            total = total + dot(tab[1, pl.ds(i * 128, 128), :], data)
+            total = total + pltpu.roll(total, 64, 1)
+            for n in range(4):
+                ob[h, i * 4 + n] = jnp.where(
+                    low16, total[32 * n : 32 * n + 16], total[32 * n + 16 : 32 * n + 32]
+                )
+
+        here = pl.ds(pl.multiple_of((sx * 32 + 4 * p + h) * 16, 16), 16)
 
         @pl.loop(1, 32)
         def _(k):
@@ -192,9 +198,9 @@
 
         db[here, :] = ob[h, (unit & 1) * 16 + (unit >> 1)]
 
-    pltpu.make_async_copy(db.at[pl.ds(0, 62 * 32)], db.at[pl.ds(0, 62 * 32)], r2).wait()
-
-    low16 = lax.broadcasted_iota(jnp.int32, (16, 128), 1) < 64
+    pltpu.make_async_copy(db.at[pl.ds(0, 124 * 16)], db.at[pl.ds(0, 124 * 16)], r2).wait()
+
+    low32 = lax.broadcasted_iota(jnp.int32, (32, 128), 1) < 64
 
     @pl.loop(0, 8)
     def _(i):
@@ -203,32 +209,27 @@
         for f in range(2):
             j = zt * 2 + f
             special = jnp.where((unit == 0) & (j == 0), 1.0, 0.0).astype(F32)
-            planes = []
-            for ri in range(2):
-                tiles = []
-                for q in range(2):
-                    ta = db[pl.ds((2 * q) * 512 + ri * 16 + j, 16, stride=32), :]
-                    tb = db[pl.ds((2 * q + 1) * 512 + ri * 16 + j, 16, stride=32), :]
-                    tiles.append(jnp.concatenate(interleave(ta, tb, low16), axis=0))
-                planes.append(jnp.concatenate(tiles, axis=1))
-            real, imag = planes
-            rh, rl = split(real)
-            ih, il = split(imag)
-            base = pl.multiple_of(j * 64, 64)
-            mh[pl.ds(base, 32), :] = rh
-            mh[pl.ds(base + 32, 32), :] = ih
-            ml[pl.ds(base, 32), :] = rl
-            ml[pl.ds(base + 32, 32), :] = il
-            sh_, sl_ = split(imag * (1.0 - special))
-            ch, cl = split(imag * special - real * (1.0 - special))
-            left_h = jnp.concatenate([rh, ih], axis=1)
-            left_l = jnp.concatenate([rl, il], axis=1)
-            right_h = jnp.concatenate(
-                [jnp.concatenate([rh, sh_], axis=1), jnp.concatenate([sh_, ch], axis=1)], axis=0
+            left, same, across = [], [], []
+            for x in range(NX):
+                tile = db[pl.ds(x * 512 + j, 32, stride=16), :]
+                turned = pltpu.roll(tile, 64, 1)
+                left.append(tile)
+                same.append(jnp.where(low32, tile, tile * (1.0 - special)))
+                across.append(
+                    jnp.where(
+                        low32,
+                        turned * (1.0 - special),
+                        tile * special - turned * (1.0 - special),
+                    )
+                )
+            left_h, left_l = split(jnp.concatenate(left, axis=1))
+            base = pl.multiple_of(j * 32, 32)
+            mh[pl.ds(base, 32), :] = left_h
+            ml[pl.ds(base, 32), :] = left_l
+            right = jnp.concatenate(
+                [jnp.concatenate(same, axis=1), jnp.concatenate(across, axis=1)], axis=0
             )
-            right_l = jnp.concatenate(
-                [jnp.concatenate([rl, sl_], axis=1), jnp.concatenate([sl_, cl], axis=1)], axis=0
-            )
+            right_h, right_l = split(right)
             grams.append(
                 dot_nt(left_h, right_h) + (dot_nt(left_h, right_l) + dot_nt(left_l, right_h))
             )
@@ -280,10 +281,11 @@
     scaled = vec * lax.rsqrt(energy + 1e-06)
     spread = scaled + pltpu.roll(scaled, 32, 1)
     spread = spread + pltpu.roll(spread, 64, 1)
-    placed = lane // 32 == row
-    vec_row = jnp.sum(jnp.where(placed, spread, 0.0), axis=0, keepdims=True)
-    energy_row = jnp.sum(jnp.where(placed, energy, 0.0), axis=0, keepdims=True)
-    message = jnp.where(row == 0, vec_row, jnp.where(row == 1, energy_row, 0.0))
+    place = (z & 1) * 2 + row // 2 == lane // 32
+    message = jnp.zeros((8, 128), F32)
+    for n, value in enumerate((spread, spread, energy, energy)):
+        chosen = jnp.where(place & (row & 1 == n % 2), value, 0.0)
+        message = jnp.where(row == n, jnp.sum(chosen, axis=0, keepdims=True), message)
     vs[...] = message
     va[z] = message
 
@@ -295,9 +297,9 @@
             device_id=((y << 4) + (zt << 1) + c, sx), device_id_type=MESH,
         ).start()
 
-    rows = lax.broadcasted_iota(jnp.int32, (64, 128), 0)
-    lanes = lax.broadcasted_iota(jnp.int32, (64, 128), 1)
-    ver, ri, j = rows // 32, (rows // 16) % 2, rows % 16
+    rows = lax.broadcasted_iota(jnp.int32, (32, 128), 0)
+    lanes = lax.broadcasted_iota(jnp.int32, (32, 128), 1)
+    ver, j = rows // 16, rows % 16
     first_unit = unit == 0
     slot = jnp.where(ver == 0, j, 15 - j)
     slot_first = jnp.where(
@@ -306,36 +308,35 @@
         jnp.where(j < 8, 8 + j, 23 - j),
     )
     slot = jnp.where(first_unit, slot_first, slot)
-    mirrored = jnp.where(first_unit, j // 8, ver) == 1
+    flip = jnp.where(jnp.where(first_unit, j // 8, ver) == 1, -1.0, 1.0)
     direct = first_unit & (ver == 0) & (j == 0)
     nyquist = first_unit & (ver == 0) & (j == 8)
-    lane_imag = (lanes // 32) % 2 == 1
-    lane_slot = lanes // 64
-    straight = jnp.where(
-        direct, jnp.where(lane_imag, 0.0, 1.0),
-        jnp.where(nyquist, jnp.where(lane_imag, 1.0, 0.0), jnp.where(lane_imag, -1.0, 1.0)),
+    alone = direct | nyquist
+    by_real = jnp.where(low32, jnp.where(nyquist, 0.0, 1.0), jnp.where(alone, 0.0, flip))
+    by_imag = jnp.where(
+        low32,
+        jnp.where(alone, jnp.where(nyquist, 1.0, 0.0), -1.0),
+        jnp.where(alone, 0.0, flip),
     )
-    straight = jnp.where(ri == 0, straight, 0.0).astype(F32)
-    across = jnp.where(direct | nyquist, 0.0, jnp.where(mirrored, -1.0, 1.0))
-    across = jnp.where(ri == 0, 0.0, across).astype(F32)
-    picked = lanes % 64 == jnp.where(nyquist, 32, 0)
+    lane_slot = lanes // 32
+    lead = lanes % 32 == 0
 
     pltpu.make_async_copy(va.at[pl.ds(0, 7)], va.at[pl.ds(0, 7)], r4).wait()
 
-    modes = jnp.zeros((64, 256), F32)
-    energies = jnp.zeros((64, 128), F32)
-    imag_row = (lax.broadcasted_iota(jnp.int32, (1, 128), 1) // 32) % 2 == 1
-    for k in range(8):
-        v = va[k, 0:1, :]
-        e = va[k, 1:2, :]
-        v_swapped = jnp.where(imag_row, pltpu.roll(v, 32, 1), pltpu.roll(v, 96, 1))
-        here = slot == 2 * k + lane_slot
-        left = jnp.where(here, straight * v + across * v_swapped, 0.0)
-        energies = energies + jnp.where(here & picked, e, 0.0)
+    modes = jnp.zeros((64, 512), F32)
+    energies = jnp.zeros((32, 128), F32)
+    for k in range(4):
+        v = va[2 * k] + va[2 * k + 1]
+        here = slot == 4 * k + lane_slot
+        left = jnp.concatenate(
+            [jnp.where(here, v[0:1, :], 0.0), jnp.where(here, v[1:2, :], 0.0)], axis=0
+        )
+        energy = jnp.where(nyquist, v[3:4, :], v[2:3, :])
+        energies = energies + jnp.where(here & lead, energy, 0.0)
         lh, ll = split(left)
         high = mh[128 * k : 128 * k + 128, :]
         modes = modes + (dot(lh, high) + (dot(lh, ml[128 * k : 128 * k + 128, :]) + dot(ll, high)))
-    energies = jnp.broadcast_to(jnp.sum(energies, axis=1, keepdims=True), (64, 128))
+    energies = jnp.broadcast_to(jnp.sum(energies, axis=1, keepdims=True), (32, 128))
 
     sends = []
     for ver in range(2):
@@ -344,19 +345,16 @@
         else:
             klass = jnp.where(unit == 0, 32, 64 - unit)
         to = bit_reverse(klass)
-        base = 32 * ver
+        base = 16 * ver
         energy_tile = jnp.where(low, energies[base : base + 8], energies[base + 8 : base + 16])
         for px in range(4):
             n = ver * 4 + px
-            q = 128 * (px // 2)
-            for ri in range(2):
-                a = modes[base + 16 * ri : base + 16 * ri + 8, q : q + 128]
-                b = modes[base + 16 * ri + 8 : base + 16 * ri + 16, q : q + 128]
-                if px % 2 == 0:
-                    tile = jnp.where(low, a, pltpu.roll(b, 64, 1))
-                else:
-                    tile = jnp.where(low, pltpu.roll(a, 64, 1), b)
-                fs[n, 8 * ri : 8 * ri + 8, :] = tile
+            real = modes[base : base + 16, 128 * px : 128 * px + 128]
+            imag = modes[base + 32 : base + 48, 128 * px : 128 * px + 128]
+            fs[n, 0:16, :] = (
+                real * by_real[base : base + 16]
+                + pltpu.roll(imag, 64, 1) * by_imag[base : base + 16]
+            )
             fs[n, 16:24, :] = energy_tile
             send = pltpu.make_async_remote_copy(
                 fs.at[n], fb.at[z], s5.at[n], r5.at[z],
@@ -385,9 +383,9 @@
     for k in range(8):
         out_ref[k] = fb[k]
 
-    for h in range(2):
+    for h in range(4):
         pltpu.make_async_copy(sb.at[h, pl.ds(0, 63)], sb.at[h, pl.ds(0, 63)], s1.at[h]).wait()
-    pltpu.make_async_copy(db.at[pl.ds(0, 62 * 32)], db.at[pl.ds(0, 62 * 32)], s2).wait()
+    pltpu.make_async_copy(db.at[pl.ds(0, 124 * 16)], db.at[pl.ds(0, 124 * 16)], s2).wait()
     pltpu.make_async_copy(gr.at[pl.ds(0, 7)], gr.at[pl.ds(0, 7)], s3).wait()
     pltpu.make_async_copy(va.at[pl.ds(0, 7)], va.at[pl.ds(0, 7)], s4).wait()
     for send, kept in sends:
@@ -400,16 +398,13 @@
 def unpack(fb, w_ref, out_ref, e_ref):
     lane = lax.broadcasted_iota(jnp.int32, (8, 128), 1)
     row = lax.broadcasted_iota(jnp.int32, (8, 128), 0)
-    low = lane < 64
+    low16 = lax.broadcasted_iota(jnp.int32, (16, 128), 1) < 64
     unscale = lax.rsqrt(w_ref[...])
     for q in range(4):
-        for ri in range(2):
-            a = fb[2 * q, 8 * ri : 8 * ri + 8, :]
-            b = fb[2 * q + 1, 8 * ri : 8 * ri + 8, :]
-            first, second = interleave(a, b, low)
-            scale = unscale[:, 128 * q : 128 * q + 128]
-            out_ref[16 * ri : 16 * ri + 8, 128 * q : 128 * q + 128] = first * scale
-            out_ref[16 * ri + 8 : 16 * ri + 16, 128 * q : 128 * q + 128] = second * scale
+        real, imag = interleave(fb[2 * q, 0:16, :], fb[2 * q + 1, 0:16, :], low16)
+        scale = unscale[:, 128 * q : 128 * q + 128]
+        out_ref[0:16, 128 * q : 128 * q + 128] = real * scale
+        out_ref[16:32, 128 * q : 128 * q + 128] = imag * scale
     tile = fb[0, 16:24, :]
     turned = pltpu.roll(tile, 64, 1)
     diagonal = jnp.where(lane == row, tile, 0.0) + jnp.where(lane == row + 8, turned, 0.0)
@@ -431,13 +426,13 @@
         scratch_shapes=[
             pltpu.VMEM((4, 512, 128), F32),
             pltpu.VMEM((2, 1024, 512), BF16),
-            pltpu.VMEM((2, 64, 16, 128), F32),
-            pltpu.VMEM((2, 64, 16, 128), F32),
-            pltpu.VMEM((2, 512, 256), BF16),
-            pltpu.VMEM((2, 32, 32, 128), F32),
+            pltpu.VMEM((4, 64, 8, 128), F32),
+            pltpu.VMEM((4, 64, 8, 128), F32),
+            pltpu.VMEM((2, 512, 128), BF16),
+            pltpu.VMEM((4, 32, 16, 128), F32),
             pltpu.VMEM((2048, 128), F32),
-            pltpu.VMEM((1024, 256), BF16),
-            pltpu.VMEM((1024, 256), BF16),
+            pltpu.VMEM((512, 512), BF16),
+            pltpu.VMEM((512, 512), BF16),
             pltpu.VMEM((8, 32, 128), F32),
             pltpu.VMEM((8, 32, 128), F32),
             pltpu.VMEM((8, 128), F32),
@@ -445,7 +440,7 @@
             pltpu.VMEM((8, 24, 128), F32),
             pltpu.VMEM((8, 24, 128), F32),
             dma((4,)), dma, pltpu.SemaphoreType.REGULAR,
-            dma((2,)), dma((2,)),
+            dma((4,)), dma((4,)),
             dma, dma, dma, dma, dma, dma,
             dma((8,)), dma((8,)),
         ],

time: 74.8 us -> 71.8 us (0.960)
  Pallas kernels: 74 us -> 71 us
    pallas_call x1, Pallas kernels: 72.4 us -> 69.4 us  [body(): pl.pallas_call(kernel, out_shape=jax.ShapeDtypeStruct((8, 24, 128), F32),...]
where the time goes in v3:
time: 71.8 us; the launch traced here: 71.7 us
  Pallas kernels  71 us (99%)
    pallas_call x1, Pallas kernels, body(): pl.pallas_call(kernel, out_shape=jax.ShapeDtypeStruct((8, 24, 128), F32),...  69.4 us
    pallas_call x1, Pallas kernels, body(): pl.pallas_call(unpack, out_shape=(jax.ShapeDtypeStruct((32, points), F32)...  1.61 us

profile of v3, /device:TPU:1, one launch (start us, length us, event | category | flops | bytes accessed | tf_op | source)
XLA Modules:
  0.0 71.7 jit_solution(7964654108039334004)
XLA Ops:
  0.6 69.4 %spod.1.fb = f32[8,24,128]{2,1,0:T(8,128)} custom-call(f32[512,512]{1,0:T(8,128)} %bitcast.4, bf16[2,1024,512]{2,1,0:T(8,128)(2,1)} %constant.2.clone.tab_hbm, f32[1,512]{1,0:T(1,128)} %bitcast.5), custom_call_target="tpu_custom_call" | custom-call | tf_op jit(solution)/shard_map/spod/pallas_call | solution.py:421
  70.0 1.6 %unpack.1 = (f32[32,512]{1,0:T(8,128)}, f32[1,16]{1,0:T(1,128)}) custom-call(f32[8,24,128]{2,1,0:T(8,128)} %spod.1.fb, f32[1,512]{1,0:T(1,128)} %bitcast.6), custom_call_target="tpu_custom_call" | custom-call | tf_op jit(solution)/shard_map/unpack/pallas_call | solution.py:450

commit v4 on v3

--- a/solution.py
+++ b/solution.py
@@ -72,7 +72,7 @@
 def kernel(
     x_hbm, tab_hbm, w_ref, out_ref,
     xin, tab, sb, rb, eh, ob, db, mh, ml, go, gr, vs, va, fs, fb,
-    in_sem, tab_sem, row_sem, s1, r1, s2, r2, s3, r3, s4, r4, s5, r5,
+    in_sem, tab_sem, step_sem, s1, r1, s2, r2, s3, r3, s4, r4, s5, r5,
 ):
     me = lax.axis_index("tm")
     sx = lax.axis_index("space")
@@ -94,14 +94,16 @@
     def greet(semaphore, tm, space):
         pl.semaphore_signal(semaphore, 1, device_id=(tm, space), device_id_type=MESH)
 
-    @pl.loop(1, 16)
-    def _(k):
-        greet(barrier, (me & 48) + ((me + k) & 15), sx)
-
-    @pl.loop(1, 4)
-    def _(k):
-        greet(barrier, (me + 16 * k) & 63, sx)
-        greet(barrier, me, (sx + k) & 3)
+    def at(dz, dc):
+        return (y << 4) + (((z + dz) & 7) << 1) + (c ^ dc)
+
+    greet(barrier, me ^ 1, sx)
+    for sign in (1, -1):
+        greet(barrier, at(sign, 0), sx)
+        greet(barrier, at(sign, 1), sx)
+        greet(barrier, (me + 16 * sign) & 63, sx)
+        greet(barrier, me, (sx + sign) & 3)
+        greet(barrier, me ^ 1, (sx + sign) & 3)
 
     def peer(k):
         return (sx + k) & 3, (y + (k >> 3)) & 3, c ^ ((k >> 2) & 1)
@@ -130,44 +132,82 @@
             t0 = xin[q, pl.ds(b, 8, stride=32), :] * factor[0][q]
             t1 = xin[q, pl.ds(256 + b, 8, stride=32), :] * factor[1][q]
             even, odd = interleave(t0, t1, low)
-            sb[b & 3, base + 4 * q] = even
-            sb[b & 3, base + 4 * q + 2] = odd
-
-    pl.semaphore_wait(barrier, 15 + 3 + 3)
-    for k in range(1, 4):
-        greet(row_sem, (me + 16 * k) & 63, sx)
-
-    def send_columns(h):
-        def send(k):
-            i = k & 7
-            dz = jnp.where((i & 1) == 1, (i + 1) >> 1, 8 - (i >> 1))
-            to = (((y + (k >> 4)) & 3) << 4) + (((z + dz) & 7) << 1) + (c ^ ((k >> 3) & 1))
-            pltpu.make_async_remote_copy(
-                sb.at[h, to], rb.at[h, me], s1.at[h], r1.at[h],
-                device_id=(to, sx), device_id_type=MESH,
-            ).start()
-
-        return send
-
-    pl.loop(1, 16)(send_columns(0))
-    pl.semaphore_wait(row_sem, 3)
-    pl.loop(16, 64)(send_columns(0))
-    for h in range(1, 4):
-        pl.loop(1, 64)(send_columns(h))
-
-    for h in range(4):
-        rb[h, me] = sb[h, me]
+            sb[base + 4 * q, b & 3] = even
+            sb[base + 4 * q + 2, b & 3] = odd
+
+    groups = (pl.ds(0, 2), pl.ds(2, 1), pl.ds(3, 1))
+
+    def send_columns(group, to):
+        pltpu.make_async_remote_copy(
+            sb.at[to, groups[group]], rb.at[me, groups[group]], s1.at[group], r1.at[group],
+            device_id=(to, sx), device_id_type=MESH,
+        ).start()
+
+    def send_row(group, offsets):
+        for dz, dc in offsets:
+            send_columns(group, at(dz, dc))
+
+    def target(k):
+        i, row_step = k & 7, k >> 4
+        dz = jnp.where((i & 1) == 1, (i + 1) >> 1, 8 - (i >> 1))
+        dy = jnp.where(row_step == 1, 1, 5 - row_step)
+        return (((y + dy) & 3) << 4) + (((z + dz) & 7) << 1) + (c ^ ((k >> 3) & 1))
+
+    near = [(1, 0), (-1, 0), (1, 1), (-1, 1), (0, 1)]
+    second = [(2, 0), (-2, 0), (2, 1), (-2, 1)]
+    far = [(3, 0), (-3, 0), (4, 0), (3, 1), (-3, 1), (4, 1)]
+
+    pl.semaphore_wait(barrier, 11)
+    for sign in (1, -1):
+        greet(step_sem.at[0], at(sign, 0), sx)
+        greet(step_sem.at[1], me, (sx + sign) & 3)
+    send_row(0, near)
+    pl.semaphore_wait(step_sem.at[0], 2)
+    for sign in (2, -2):
+        greet(step_sem.at[2], at(sign, 0), sx)
+    send_row(0, second)
+    send_row(1, near)
+    send_row(2, near)
+    pl.semaphore_wait(step_sem.at[2], 2)
+    pl.semaphore_wait(step_sem.at[1], 2)
+    for sign in (1, -1):
+        greet(step_sem.at[3], (me + 16 * sign) & 63, sx)
+    send_row(0, far)
+    pl.semaphore_wait(step_sem.at[3], 2)
+    for sign in (1, -1):
+        greet(step_sem.at[4], (me + 16 * sign) & 63, sx)
+
+    @pl.loop(16, 48)
+    def _(k):
+        send_columns(0, target(k))
+
+    pl.semaphore_wait(step_sem.at[4], 2)
+
+    @pl.loop(48, 64)
+    def _(k):
+        send_columns(0, target(k))
+
+    for group in (1, 2):
+        send_row(group, second + far)
+
+        @pl.loop(16, 64)
+        def _(k):
+            send_columns(group, target(k))
+
+    rb[me] = sb[me]
 
     load_tab.wait()
     low64 = lax.broadcasted_iota(jnp.int32, (64, 128), 1) < 64
     low16 = lax.broadcasted_iota(jnp.int32, (16, 128), 1) < 64
     for h in range(4):
-        pltpu.make_async_copy(rb.at[h, pl.ds(0, 63)], rb.at[h, pl.ds(0, 63)], r1.at[h]).wait()
+        if h != 1:
+            landed = rb.at[pl.ds(0, 63), groups[max(h - 1, 0)]]
+            pltpu.make_async_copy(landed, landed, r1.at[max(h - 1, 0)]).wait()
 
         @pl.loop(0, 4)
         def _(i):
-            first = rb[h, pl.ds(i * 8, 8)].reshape(64, 128)
-            second = rb[h, pl.ds(32 + i * 8, 8)].reshape(64, 128)
+            first = rb[pl.ds(i * 8, 8), h].reshape(64, 128)
+            second = rb[pl.ds(32 + i * 8, 8), h].reshape(64, 128)
             for parity, value in enumerate((first + second, first - second)):
                 high = value.astype(BF16).astype(F32)
                 early, late = interleave(high, value - high, low64)
@@ -383,8 +423,9 @@
     for k in range(8):
         out_ref[k] = fb[k]
 
-    for h in range(4):
-        pltpu.make_async_copy(sb.at[h, pl.ds(0, 63)], sb.at[h, pl.ds(0, 63)], s1.at[h]).wait()
+    for group in range(3):
+        left = sb.at[pl.ds(0, 63), groups[group]]
+        pltpu.make_async_copy(left, left, s1.at[group]).wait()
     pltpu.make_async_copy(db.at[pl.ds(0, 124 * 16)], db.at[pl.ds(0, 124 * 16)], s2).wait()
     pltpu.make_async_copy(gr.at[pl.ds(0, 7)], gr.at[pl.ds(0, 7)], s3).wait()
     pltpu.make_async_copy(va.at[pl.ds(0, 7)], va.at[pl.ds(0, 7)], s4).wait()
@@ -420,14 +461,14 @@
     weights = quad_weights.reshape(1, points)
     packed = pl.pallas_call(
         kernel,
-        out_shape=jax.ShapeDtypeStruct((8, 24, 128), F32),
+        out_shape=pltpu.VMEM((8, 24, 128), F32),
         in_specs=[any_spec, any_spec, vmem],
         out_specs=vmem,
         scratch_shapes=[
             pltpu.VMEM((4, 512, 128), F32),
             pltpu.VMEM((2, 1024, 512), BF16),
-            pltpu.VMEM((4, 64, 8, 128), F32),
-            pltpu.VMEM((4, 64, 8, 128), F32),
+            pltpu.VMEM((64, 4, 8, 128), F32),
+            pltpu.VMEM((64, 4, 8, 128), F32),
             pltpu.VMEM((2, 512, 128), BF16),
             pltpu.VMEM((4, 32, 16, 128), F32),
             pltpu.VMEM((2048, 128), F32),
@@ -439,8 +480,8 @@
             pltpu.VMEM((8, 8, 128), F32),
             pltpu.VMEM((8, 24, 128), F32),
             pltpu.VMEM((8, 24, 128), F32),
-            dma((4,)), dma, pltpu.SemaphoreType.REGULAR,
-            dma((4,)), dma((4,)),
+            dma((4,)), dma, pltpu.SemaphoreType.REGULAR((5,)),
+            dma((3,)), dma((3,)),
             dma, dma, dma, dma, dma, dma,
             dma((8,)), dma((8,)),
         ],
@@ -456,7 +497,7 @@
         in_specs=[vmem, vmem],
         out_specs=(vmem, vmem),
         name="unpack",
-    )(packed, weights)
+    )(pltpu.with_memory_space_constraint(packed, pltpu.VMEM), weights)
     return modes.reshape(2, 16, points), energies.reshape(16)
 
 

time: 71.8 us -> 73.3 us (1.021)
  Pallas kernels: 71 us -> 72.5 us
    pallas_call x1, Pallas kernels: 69.4 us -> 71.1 us  [body(): pl.pallas_call(kernel, out_shape=pltpu.VMEM((8, 24, 128), F32), in_specs=...]
where the time goes in v4:
time: 73.3 us; the launch traced here: 73.2 us
  Pallas kernels  72.5 us (99%)
    pallas_call x1, Pallas kernels, body(): pl.pallas_call(kernel, out_shape=pltpu.VMEM((8, 24, 128), F32), in_specs=...  71.1 us

profile of v4, /device:TPU:1, one launch (start us, length us, event | category | flops | bytes accessed | tf_op | source)
XLA Modules:
  0.0 73.2 jit_solution(7555661536141928110)
XLA Ops:
  0.6 71.1 %spod.1.fb = f32[8,24,128]{2,1,0:T(8,128)S(1)} custom-call(f32[512,512]{1,0:T(8,128)} %bitcast.4, bf16[2,1024,512]{2,1,0:T(8,128)(2,1)} %constant.2.clone.tab_hbm, f32[1,512]{1,0:T(1,128)} %bitcast.5), custom_call_target="tpu_custom_call" | custom-call | tf_op jit(solution)/shard_map/spod/pallas_call | solution.py:462
  71.8 1.4 %unpack.1 = (f32[32,512]{1,0:T(8,128)}, f32[1,16]{1,0:T(1,128)}) custom-call(f32[8,24,128]{2,1,0:T(8,128)S(1)} %spod.1.fb, f32[1,512]{1,0:T(1,128)} %bitcast.6), custom_call_target="tpu_custom_call" | custom-call | tf_op jit(solution)/shard_map/unpack/pallas_call | solution.py:491

commit v5 on v4

--- a/solution.py
+++ b/solution.py
@@ -12,7 +12,6 @@
 F32 = jnp.float32
 BF16 = jnp.bfloat16
 MESH = pl.DeviceIdType.MESH
-HIGHEST = lax.Precision.HIGHEST
 NT = 1024
 NX, NY, NZ, NC = 4, 4, 8, 2
 
@@ -33,7 +32,7 @@
     table = np.concatenate(rows).astype(np.float32)
     high = table.astype(jnp.bfloat16)
     low = (table - high.astype(np.float32)).astype(jnp.bfloat16)
-    return np.stack([high, low])
+    return np.stack([high.reshape(2, 512, 512), low.reshape(2, 512, 512)], axis=1).reshape(2, 1024, 512)
 
 
 def split(x):
@@ -94,19 +93,20 @@
     def greet(semaphore, tm, space):
         pl.semaphore_signal(semaphore, 1, device_id=(tm, space), device_id_type=MESH)
 
-    def at(dz, dc):
-        return (y << 4) + (((z + dz) & 7) << 1) + (c ^ dc)
-
-    greet(barrier, me ^ 1, sx)
-    for sign in (1, -1):
-        greet(barrier, at(sign, 0), sx)
-        greet(barrier, at(sign, 1), sx)
-        greet(barrier, (me + 16 * sign) & 63, sx)
-        greet(barrier, me, (sx + sign) & 3)
-        greet(barrier, me ^ 1, (sx + sign) & 3)
+    @pl.loop(1, 16)
+    def _(k):
+        greet(barrier, (me & 48) + ((me + k) & 15), sx)
+
+    @pl.loop(1, 4)
+    def _(k):
+        greet(barrier, (me + 16 * k) & 63, sx)
+        greet(barrier, me, (sx + k) & 3)
 
     def peer(k):
-        return (sx + k) & 3, (y + (k >> 3)) & 3, c ^ ((k >> 2) & 1)
+        dx, dy = k & 3, k >> 3
+        dx = jnp.where(dx < 2, 2 - dx, 3 * (3 - dx))
+        dy = jnp.where(dy < 2, 2 - dy, 3 * (3 - dy))
+        return (sx + dx) & 3, (y + dy) & 3, c ^ 1 ^ ((k >> 2) & 1)
 
     lane = lax.broadcasted_iota(jnp.int32, (8, 128), 1)
     row = lax.broadcasted_iota(jnp.int32, (8, 128), 0)
@@ -143,56 +143,33 @@
             device_id=(to, sx), device_id_type=MESH,
         ).start()
 
-    def send_row(group, offsets):
-        for dz, dc in offsets:
-            send_columns(group, at(dz, dc))
-
     def target(k):
-        i, row_step = k & 7, k >> 4
+        i = k & 7
         dz = jnp.where((i & 1) == 1, (i + 1) >> 1, 8 - (i >> 1))
-        dy = jnp.where(row_step == 1, 1, 5 - row_step)
-        return (((y + dy) & 3) << 4) + (((z + dz) & 7) << 1) + (c ^ ((k >> 3) & 1))
-
-    near = [(1, 0), (-1, 0), (1, 1), (-1, 1), (0, 1)]
-    second = [(2, 0), (-2, 0), (2, 1), (-2, 1)]
-    far = [(3, 0), (-3, 0), (4, 0), (3, 1), (-3, 1), (4, 1)]
-
-    pl.semaphore_wait(barrier, 11)
-    for sign in (1, -1):
-        greet(step_sem.at[0], at(sign, 0), sx)
-        greet(step_sem.at[1], me, (sx + sign) & 3)
-    send_row(0, near)
-    pl.semaphore_wait(step_sem.at[0], 2)
-    for sign in (2, -2):
-        greet(step_sem.at[2], at(sign, 0), sx)
-    send_row(0, second)
-    send_row(1, near)
-    send_row(2, near)
-    pl.semaphore_wait(step_sem.at[2], 2)
-    pl.semaphore_wait(step_sem.at[1], 2)
-    for sign in (1, -1):
-        greet(step_sem.at[3], (me + 16 * sign) & 63, sx)
-    send_row(0, far)
-    pl.semaphore_wait(step_sem.at[3], 2)
-    for sign in (1, -1):
-        greet(step_sem.at[4], (me + 16 * sign) & 63, sx)
-
-    @pl.loop(16, 48)
+        to = (((y + (k >> 4)) & 3) << 4) + (((z + dz) & 7) << 1)
+        return to + (c ^ ((k >> 3) & 1))
+
+    def send_rest(group):
+        @pl.loop(1, 64)
+        def _(k):
+            send_columns(group, target(64 - k))
+
+    pl.semaphore_wait(barrier, 15 + 3 + 3)
+    for k in range(1, 4):
+        greet(step_sem, (me + 16 * k) & 63, sx)
+
+    @pl.loop(1, 16)
     def _(k):
         send_columns(0, target(k))
 
-    pl.semaphore_wait(step_sem.at[4], 2)
-
-    @pl.loop(48, 64)
+    pl.semaphore_wait(step_sem, 3)
+
+    @pl.loop(16, 64)
     def _(k):
         send_columns(0, target(k))
 
-    for group in (1, 2):
-        send_row(group, second + far)
-
-        @pl.loop(16, 64)
-        def _(k):
-            send_columns(group, target(k))
+    send_rest(1)
+    send_rest(2)
 
     rb[me] = sb[me]
 
@@ -214,20 +191,19 @@
                 eh[parity, pl.ds(i * 64, 64), :] = early.astype(BF16)
                 eh[parity, pl.ds(256 + i * 64, 64), :] = late.astype(BF16)
 
-        @pl.loop(0, 8)
-        def _(i):
-            data = eh[i >> 2]
-            total = dot(tab[0, pl.ds(i * 128, 128), :], data)
-            total = total + dot(tab[1, pl.ds(i * 128, 128), :], data)
+        @pl.loop(0, 2)
+        def _(parity):
+            product = dot(tab[parity], eh[parity])
+            total = product[0:512] + product[512:1024]
             total = total + pltpu.roll(total, 64, 1)
-            for n in range(4):
-                ob[h, i * 4 + n] = jnp.where(
+            for n in range(16):
+                ob[h, parity * 16 + n] = jnp.where(
                     low16, total[32 * n : 32 * n + 16], total[32 * n + 16 : 32 * n + 32]
                 )
 
         here = pl.ds(pl.multiple_of((sx * 32 + 4 * p + h) * 16, 16), 16)
 
-        @pl.loop(1, 32)
+        @pl.loop(0, 31)
         def _(k):
             px, py, pc = peer(k)
             g = unit_of(px, py, pc)
@@ -248,32 +224,34 @@
         grams = []
         for f in range(2):
             j = zt * 2 + f
-            special = jnp.where((unit == 0) & (j == 0), 1.0, 0.0).astype(F32)
-            left, same, across = [], [], []
-            for x in range(NX):
-                tile = db[pl.ds(x * 512 + j, 32, stride=16), :]
-                turned = pltpu.roll(tile, 64, 1)
-                left.append(tile)
-                same.append(jnp.where(low32, tile, tile * (1.0 - special)))
-                across.append(
-                    jnp.where(
-                        low32,
-                        turned * (1.0 - special),
-                        tile * special - turned * (1.0 - special),
-                    )
-                )
-            left_h, left_l = split(jnp.concatenate(left, axis=1))
+            keep = jnp.where((unit == 0) & (j == 0), 0.0, 1.0).astype(F32)
+            real, imag = [], []
+            for x in range(0, NX, 2):
+                first = db[pl.ds(x * 512 + j, 32, stride=16), :]
+                second = db[pl.ds(x * 512 + 512 + j, 32, stride=16), :]
+                r, m = interleave(first, second, low32)
+                real.append(r)
+                imag.append(m)
+            real_h, real_l = split(jnp.concatenate(real, axis=1))
+            imag_h, imag_l = split(jnp.concatenate(imag, axis=1))
+            left_h = jnp.concatenate([real_h, imag_h], axis=1)
+            left_l = jnp.concatenate([real_l, imag_l], axis=1)
             base = pl.multiple_of(j * 32, 32)
             mh[pl.ds(base, 32), :] = left_h
             ml[pl.ds(base, 32), :] = left_l
-            right = jnp.concatenate(
-                [jnp.concatenate(same, axis=1), jnp.concatenate(across, axis=1)], axis=0
+            lone_part = (1.0 - keep).astype(BF16)
+            keep = keep.astype(BF16)
+            right = []
+            for r, m in ((real_h, imag_h), (real_l, imag_l)):
+                kept = m * keep
+                right.append(jnp.concatenate([r, kept], axis=1))
+                right.append(jnp.concatenate([kept, m * lone_part - r * keep], axis=1))
+            product = dot_nt(
+                jnp.concatenate([left_h, left_l], axis=0), jnp.concatenate(right, axis=0)
             )
-            right_h, right_l = split(right)
-            grams.append(
-                dot_nt(left_h, right_h) + (dot_nt(left_h, right_l) + dot_nt(left_l, right_h))
-            )
-        pair = jnp.concatenate(grams, axis=1)
+            total = product[0:32] + product[32:64]
+            grams.append(total + pltpu.roll(total, 64, 1))
+        pair = jnp.where(low32, grams[0], grams[1])
 
         @pl.when(i < 7)
         def _():
@@ -291,7 +269,8 @@
     gram = gr[0]
     for k in range(1, 8):
         gram = gram + gr[k]
-    gram = gram * (1.0 / 2048.0)
+    gram_h, gram_l = split(gram * (1.0 / 2048.0))
+    gram = jnp.concatenate([gram_h, gram_l], axis=1)
 
     even = row % 2 == 0
     lone = (row < 2) & (unit == 0) & (z == 0)
@@ -301,7 +280,11 @@
         return jnp.where(even, pltpu.roll(v, 7, 0), pltpu.roll(v, 1, 0))
 
     def image_of(v):
-        product = jnp.dot(v[:, 0:32], gram, preferred_element_type=F32, precision=HIGHEST)
+        high = v.astype(BF16).astype(F32)
+        both = jnp.where(row < 4, high, pltpu.roll(v - high, 4, 0)).astype(BF16)
+        product = dot(both[:, 0:32], gram)
+        product = product[:, 0:128] + product[:, 128:256]
+        product = product + pltpu.roll(product, 4, 0)
         chosen = jnp.where(row < 2, product, pltpu.roll(product, 64, 1))
         other = pltpu.roll(chosen, 96, 1)
         crossed = swap_rows(other)
@@ -352,12 +335,9 @@
     direct = first_unit & (ver == 0) & (j == 0)
     nyquist = first_unit & (ver == 0) & (j == 8)
     alone = direct | nyquist
-    by_real = jnp.where(low32, jnp.where(nyquist, 0.0, 1.0), jnp.where(alone, 0.0, flip))
-    by_imag = jnp.where(
-        low32,
-        jnp.where(alone, jnp.where(nyquist, 1.0, 0.0), -1.0),
-        jnp.where(alone, 0.0, flip),
-    )
+    real_by_real = jnp.where(nyquist, 0.0, 1.0)
+    real_by_imag = jnp.where(direct, 0.0, jnp.where(nyquist, 1.0, -1.0))
+    imag_by_any = jnp.where(alone, 0.0, flip)
     lane_slot = lanes // 32
     lead = lanes % 32 == 0
 
@@ -389,12 +369,21 @@
         energy_tile = jnp.where(low, energies[base : base + 8], energies[base + 8 : base + 16])
         for px in range(4):
             n = ver * 4 + px
-            real = modes[base : base + 16, 128 * px : 128 * px + 128]
-            imag = modes[base + 32 : base + 48, 128 * px : 128 * px + 128]
-            fs[n, 0:16, :] = (
-                real * by_real[base : base + 16]
-                + pltpu.roll(imag, 64, 1) * by_imag[base : base + 16]
+            at_real = 128 * (px // 2)
+            at_imag = 256 + at_real
+            part = slice(base, base + 16)
+            twin = slice(base + 32, base + 48)
+            real = (
+                modes[part, at_real : at_real + 128] * real_by_real[part]
+                + modes[twin, at_imag : at_imag + 128] * real_by_imag[part]
             )
+            imag = (
+                modes[part, at_imag : at_imag + 128] + modes[twin, at_real : at_real + 128]
+            ) * imag_by_any[part]
+            if px % 2 == 0:
+                fs[n, 0:16, :] = jnp.where(low16, real, pltpu.roll(imag, 64, 1))
+            else:
+                fs[n, 0:16, :] = jnp.where(low16, pltpu.roll(real, 64, 1), imag)
             fs[n, 16:24, :] = energy_tile
             send = pltpu.make_async_remote_copy(
                 fs.at[n], fb.at[z], s5.at[n], r5.at[z],
@@ -480,7 +469,7 @@
             pltpu.VMEM((8, 8, 128), F32),
             pltpu.VMEM((8, 24, 128), F32),
             pltpu.VMEM((8, 24, 128), F32),
-            dma((4,)), dma, pltpu.SemaphoreType.REGULAR((5,)),
+            dma((4,)), dma, pltpu.SemaphoreType.REGULAR,
             dma((3,)), dma((3,)),
             dma, dma, dma, dma, dma, dma,
             dma((8,)), dma((8,)),

time: 73.3 us -> 68.2 us (0.930)
  Pallas kernels: 72.5 us -> 67.5 us
    pallas_call x1, Pallas kernels: 71.1 us -> 66.1 us  [body(): pl.pallas_call(kernel, out_shape=pltpu.VMEM((8, 24, 128), F32), in_specs=...]
where the time goes in v5:
time: 68.2 us; the launch traced here: 68.1 us
  Pallas kernels  67.5 us (99%)
    pallas_call x1, Pallas kernels, body(): pl.pallas_call(kernel, out_shape=pltpu.VMEM((8, 24, 128), F32), in_specs=...  66.1 us
    pallas_call x1, Pallas kernels, body(): pl.pallas_call(unpack, out_shape=(jax.ShapeDtypeStruct((32, points), F32)...  1.4 us

profile of v5, /device:TPU:1, one launch (start us, length us, event | category | flops | bytes accessed | tf_op | source)
XLA Modules:
  0.0 68.1 jit_solution(10575802033898522178)
XLA Ops:
  0.6 66.1 %spod.1.fb = f32[8,24,128]{2,1,0:T(8,128)S(1)} custom-call(f32[512,512]{1,0:T(8,128)} %bitcast.4, bf16[2,1024,512]{2,1,0:T(8,128)(2,1)} %constant.2.clone.tab_hbm, f32[1,512]{1,0:T(1,128)} %bitcast.5), custom_call_target="tpu_custom_call" | custom-call | tf_op jit(solution)/shard_map/spod/pallas_call | solution.py:451
  66.7 1.4 %unpack.1 = (f32[32,512]{1,0:T(8,128)}, f32[1,16]{1,0:T(1,128)}) custom-call(f32[8,24,128]{2,1,0:T(8,128)S(1)} %spod.1.fb, f32[1,512]{1,0:T(1,128)} %bitcast.6), custom_call_target="tpu_custom_call" | custom-call | tf_op jit(solution)/shard_map/unpack/pallas_call | solution.py:480

commit v6 on v5

--- a/solution.py
+++ b/solution.py
@@ -69,9 +69,9 @@
 
 
 def kernel(
-    x_hbm, tab_hbm, w_ref, out_ref,
-    xin, tab, sb, rb, eh, ob, db, mh, ml, go, gr, vs, va, fs, fb,
-    in_sem, tab_sem, step_sem, s1, r1, s2, r2, s3, r3, s4, r4, s5, r5,
+    x_hbm, tab_hbm, w_hbm, out_ref, e_ref,
+    xin, w_ref, tab, sb, rb, eh, ob, db, mh, ml, go, gr, vs, va, fs, fb,
+    in_sem, w_sem, tab_sem, step_sem, s1, r1, s2, r2, s3, r3, s4, r4, s5, r5,
 ):
     me = lax.axis_index("tm")
     sx = lax.axis_index("space")
@@ -85,33 +85,31 @@
     ]
     for load in loads:
         load.start()
+    load_w = pltpu.make_async_copy(w_hbm, w_ref, w_sem)
+    load_w.start()
     load_tab = pltpu.make_async_copy(tab_hbm, tab, tab_sem)
-    load_tab.start()
 
     barrier = pltpu.get_barrier_semaphore()
 
     def greet(semaphore, tm, space):
         pl.semaphore_signal(semaphore, 1, device_id=(tm, space), device_id_type=MESH)
 
-    @pl.loop(1, 16)
+    @pl.loop(0, 15)
     def _(k):
-        greet(barrier, (me & 48) + ((me + k) & 15), sx)
+        greet(barrier, (me & 48) + (far_first(z, k >> 1) << 1) + (c ^ 1 ^ (k & 1)), sx)
 
     @pl.loop(1, 4)
     def _(k):
         greet(barrier, (me + 16 * k) & 63, sx)
         greet(barrier, me, (sx + k) & 3)
 
-    def peer(k):
-        dx, dy = k & 3, k >> 3
-        dx = jnp.where(dx < 2, 2 - dx, 3 * (3 - dx))
-        dy = jnp.where(dy < 2, 2 - dy, 3 * (3 - dy))
-        return (sx + dx) & 3, (y + dy) & 3, c ^ 1 ^ ((k >> 2) & 1)
-
     lane = lax.broadcasted_iota(jnp.int32, (8, 128), 1)
     row = lax.broadcasted_iota(jnp.int32, (8, 128), 0)
     low = lane < 64
+    load_tab.start()
+    load_w.wait()
     root_w = jnp.sqrt(w_ref[...])
+    unscale = lax.rsqrt(w_ref[...])
     for load in loads:
         load.wait()
     factor = []
@@ -191,8 +189,12 @@
                 eh[parity, pl.ds(i * 64, 64), :] = early.astype(BF16)
                 eh[parity, pl.ds(256 + i * 64, 64), :] = late.astype(BF16)
 
+        here = pl.ds(pl.multiple_of((sx * 32 + 4 * p + h) * 16, 16), 16)
+
         @pl.loop(0, 2)
-        def _(parity):
+        def _(step):
+            first_y = y ^ 2 ^ (3 * step)
+            parity = first_y >> 1
             product = dot(tab[parity], eh[parity])
             total = product[0:512] + product[512:1024]
             total = total + pltpu.roll(total, 64, 1)
@@ -201,16 +203,16 @@
                     low16, total[32 * n : 32 * n + 16], total[32 * n + 16 : 32 * n + 32]
                 )
 
-        here = pl.ds(pl.multiple_of((sx * 32 + 4 * p + h) * 16, 16), 16)
-
-        @pl.loop(0, 31)
-        def _(k):
-            px, py, pc = peer(k)
-            g = unit_of(px, py, pc)
-            pltpu.make_async_remote_copy(
-                ob.at[h, (g & 1) * 16 + (g >> 1)], db.at[here], s2, r2,
-                device_id=((py << 4) + (z << 1) + pc, px), device_id_type=MESH,
-            ).start()
+            @pl.loop(0, 16 - step)
+            def _(k):
+                dx = k & 3
+                dx = jnp.where(dx < 2, 2 - dx, 3 * (3 - dx))
+                px, py, pc = (sx + dx) & 3, first_y ^ (k >> 3), c ^ 1 ^ ((k >> 2) & 1)
+                g = unit_of(px, py, pc)
+                pltpu.make_async_remote_copy(
+                    ob.at[h, (g & 1) * 16 + (g >> 1)], db.at[here], s2, r2,
+                    device_id=((py << 4) + (z << 1) + pc, px), device_id_type=MESH,
+                ).start()
 
         db[here, :] = ob[h, (unit & 1) * 16 + (unit >> 1)]
 
@@ -343,19 +345,21 @@
 
     pltpu.make_async_copy(va.at[pl.ds(0, 7)], va.at[pl.ds(0, 7)], r4).wait()
 
-    modes = jnp.zeros((64, 512), F32)
     energies = jnp.zeros((32, 128), F32)
+    lefts = []
     for k in range(4):
         v = va[2 * k] + va[2 * k + 1]
         here = slot == 4 * k + lane_slot
-        left = jnp.concatenate(
-            [jnp.where(here, v[0:1, :], 0.0), jnp.where(here, v[1:2, :], 0.0)], axis=0
+        lefts.append(
+            jnp.concatenate(
+                [jnp.where(here, v[0:1, :], 0.0), jnp.where(here, v[1:2, :], 0.0)], axis=0
+            )
         )
         energy = jnp.where(nyquist, v[3:4, :], v[2:3, :])
         energies = energies + jnp.where(here & lead, energy, 0.0)
-        lh, ll = split(left)
-        high = mh[128 * k : 128 * k + 128, :]
-        modes = modes + (dot(lh, high) + (dot(lh, ml[128 * k : 128 * k + 128, :]) + dot(ll, high)))
+    lh, ll = split(jnp.concatenate(lefts, axis=1))
+    modes = dot(jnp.concatenate([lh, ll], axis=0), mh[...])
+    modes = modes[0:64] + (modes[64:128] + dot(lh, ml[...]))
     energies = jnp.broadcast_to(jnp.sum(energies, axis=1, keepdims=True), (32, 128))
 
     sends = []
@@ -409,27 +413,6 @@
         def _():
             pltpu.make_async_copy(fb.at[k], fb.at[k], r5.at[k]).wait()
 
-    for k in range(8):
-        out_ref[k] = fb[k]
-
-    for group in range(3):
-        left = sb.at[pl.ds(0, 63), groups[group]]
-        pltpu.make_async_copy(left, left, s1.at[group]).wait()
-    pltpu.make_async_copy(db.at[pl.ds(0, 124 * 16)], db.at[pl.ds(0, 124 * 16)], s2).wait()
-    pltpu.make_async_copy(gr.at[pl.ds(0, 7)], gr.at[pl.ds(0, 7)], s3).wait()
-    pltpu.make_async_copy(va.at[pl.ds(0, 7)], va.at[pl.ds(0, 7)], s4).wait()
-    for send, kept in sends:
-
-        @pl.when(jnp.logical_not(kept))
-        def _():
-            send.wait_send()
-
-
-def unpack(fb, w_ref, out_ref, e_ref):
-    lane = lax.broadcasted_iota(jnp.int32, (8, 128), 1)
-    row = lax.broadcasted_iota(jnp.int32, (8, 128), 0)
-    low16 = lax.broadcasted_iota(jnp.int32, (16, 128), 1) < 64
-    unscale = lax.rsqrt(w_ref[...])
     for q in range(4):
         real, imag = interleave(fb[2 * q, 0:16, :], fb[2 * q + 1, 0:16, :], low16)
         scale = unscale[:, 128 * q : 128 * q + 128]
@@ -440,6 +423,29 @@
     diagonal = jnp.where(lane == row, tile, 0.0) + jnp.where(lane == row + 8, turned, 0.0)
     e_ref[...] = jnp.sum(diagonal, axis=0, keepdims=True)[:, 0:16]
 
+    for group in range(3):
+        left = sb.at[pl.ds(0, 63), groups[group]]
+        pltpu.make_async_copy(left, left, s1.at[group]).wait()
+    pltpu.make_async_copy(db.at[pl.ds(0, 124 * 16)], db.at[pl.ds(0, 124 * 16)], s2).wait()
+    pltpu.make_async_copy(gr.at[pl.ds(0, 7)], gr.at[pl.ds(0, 7)], s3).wait()
+    pltpu.make_async_copy(va.at[pl.ds(0, 7)], va.at[pl.ds(0, 7)], s4).wait()
+    for send, kept in sends:
+
+        @pl.when(jnp.logical_not(kept))
+        def _():
+            send.wait_send()
+
+
+def hand_over(modes_ref, e_ref, modes_hbm, e_hbm, sem):
+    copies = [
+        pltpu.make_async_copy(modes_ref, modes_hbm, sem.at[0]),
+        pltpu.make_async_copy(e_ref, e_hbm, sem.at[1]),
+    ]
+    for copy in copies:
+        copy.start()
+    for copy in copies:
+        copy.wait()
+
 
 def body(snapshots, quad_weights):
     times, blocks, points = snapshots.shape
@@ -448,13 +454,14 @@
     vmem = pl.BlockSpec(memory_space=pltpu.VMEM)
     dma = pltpu.SemaphoreType.DMA
     weights = quad_weights.reshape(1, points)
-    packed = pl.pallas_call(
+    modes, energies = pl.pallas_call(
         kernel,
-        out_shape=pltpu.VMEM((8, 24, 128), F32),
-        in_specs=[any_spec, any_spec, vmem],
-        out_specs=vmem,
+        out_shape=(pltpu.VMEM((32, 512), F32), pltpu.VMEM((1, 16), F32)),
+        in_specs=[any_spec, any_spec, any_spec],
+        out_specs=(vmem, vmem),
         scratch_shapes=[
             pltpu.VMEM((4, 512, 128), F32),
+            pltpu.VMEM((1, 512), F32),
             pltpu.VMEM((2, 1024, 512), BF16),
             pltpu.VMEM((64, 4, 8, 128), F32),
             pltpu.VMEM((64, 4, 8, 128), F32),
@@ -469,7 +476,7 @@
             pltpu.VMEM((8, 8, 128), F32),
             pltpu.VMEM((8, 24, 128), F32),
             pltpu.VMEM((8, 24, 128), F32),
-            dma((4,)), dma, pltpu.SemaphoreType.REGULAR,
+            dma((4,)), dma, dma, pltpu.SemaphoreType.REGULAR,
             dma((3,)), dma((3,)),
             dma, dma, dma, dma, dma, dma,
             dma((8,)), dma((8,)),
@@ -478,15 +485,19 @@
         name="spod",
     )(snapshots.reshape(times * blocks, points), table, weights)
     modes, energies = pl.pallas_call(
-        unpack,
+        hand_over,
         out_shape=(
             jax.ShapeDtypeStruct((32, points), F32),
             jax.ShapeDtypeStruct((1, 16), F32),
         ),
         in_specs=[vmem, vmem],
-        out_specs=(vmem, vmem),
-        name="unpack",
-    )(pltpu.with_memory_space_constraint(packed, pltpu.VMEM), weights)
+        out_specs=(any_spec, any_spec),
+        scratch_shapes=[dma((2,))],
+        name="hand_over",
+    )(
+        pltpu.with_memory_space_constraint(modes, pltpu.VMEM),
+        pltpu.with_memory_space_constraint(energies, pltpu.VMEM),
+    )
     return modes.reshape(2, 16, points), energies.reshape(16)
 
 

time: 68.2 us -> 66.5 us (0.975)
  Pallas kernels: 67.5 us -> 65.8 us
    pallas_call x2, Pallas kernels: 67.5 us -> 65.8 us  [the longest x1 65.2 us: body(): pl.pallas_call(kernel, out_shape=(pltpu.VMEM((32, 512), F32), pltpu.VMEM(...]
where the time goes in v6:
time: 66.5 us
  Pallas kernels  65.8 us (99%)
    pallas_call x1, Pallas kernels, body(): pl.pallas_call(kernel, out_shape=(pltpu.VMEM((32, 512), F32), pltpu.VMEM(...  65.2 us

profile of v6, /device:TPU:1, one launch (start us, length us, event | category | flops | bytes accessed | tf_op | source)
XLA Modules:
  0.0 66.5 jit_solution(10487414151856362620)
XLA Ops:
  0.6 65.2 %spod.1 = (f32[32,512]{1,0:T(8,128)S(1)}, f32[1,16]{1,0:T(1,128)S(1)}) custom-call(f32[512,512]{1,0:T(8,128)} %bitcast.4, bf16[2,1024,512]{2,1,0:T(8,128)(2,1)} %constant.2.clone.tab_hbm, f32[1,512]{1,0:T(1,128)} %bitcast.5), custom_call_target="tpu_custom_call" | custom-call | tf_op jit(solution)/shard_map/spod/pallas_call | solution.py:457
  65.8 0.7 hand_over.1

commit v7 on v6

--- a/solution.py
+++ b/solution.py
@@ -1,3 +1,4 @@
+import functools
 import math
 
 import jax
@@ -122,16 +123,19 @@
         window = cosine * cosine * (1.0 / math.sqrt(0.375 * NT))
         factor.append([window * root_w[:, 128 * q : 128 * q + 128] for q in range(4)])
 
-    @pl.loop(0, 32)
-    def _(b):
-        owner = b >> 2
+    def arrange(half, n):
+        owner = n >> 1
+        chunk = half * 2 + (n & 1)
+        b = owner * 4 + chunk
         base = (owner >> 1) * 16 + (owner & 1)
         for q in range(4):
             t0 = xin[q, pl.ds(b, 8, stride=32), :] * factor[0][q]
             t1 = xin[q, pl.ds(256 + b, 8, stride=32), :] * factor[1][q]
             even, odd = interleave(t0, t1, low)
-            sb[base + 4 * q, b & 3] = even
-            sb[base + 4 * q + 2, b & 3] = odd
+            sb[base + 4 * q, chunk] = even
+            sb[base + 4 * q + 2, chunk] = odd
+
+    pl.loop(0, 16)(functools.partial(arrange, 0))
 
     groups = (pl.ds(0, 2), pl.ds(2, 1), pl.ds(3, 1))
 
@@ -160,6 +164,7 @@
     def _(k):
         send_columns(0, target(k))
 
+    pl.loop(0, 16)(functools.partial(arrange, 1))
     pl.semaphore_wait(step_sem, 3)
 
     @pl.loop(16, 64)

time: 66.5 us -> 65.4 us (0.983)
  Pallas kernels: 65.8 us -> 64.7 us
    pallas_call x1, Pallas kernels: 65.2 us -> 64 us  [body(): pl.pallas_call(kernel, out_shape=(pltpu.VMEM((32, 512), F32), pltpu.VMEM(...]
where the time goes in v7:
time: 65.4 us; the launch traced here: 65.3 us
  Pallas kernels  64.7 us (99%)
    pallas_call x1, Pallas kernels, body(): pl.pallas_call(kernel, out_shape=(pltpu.VMEM((32, 512), F32), pltpu.VMEM(...  64 us

profile of v7, /device:TPU:1, one launch (start us, length us, event | category | flops | bytes accessed | tf_op | source)
XLA Modules:
  0.0 65.3 jit_solution(930236415869065585)
XLA Ops:
  0.6 64.0 %spod.1 = (f32[32,512]{1,0:T(8,128)S(1)}, f32[1,16]{1,0:T(1,128)S(1)}) custom-call(f32[512,512]{1,0:T(8,128)} %bitcast.4, bf16[2,1024,512]{2,1,0:T(8,128)(2,1)} %constant.2.clone.tab_hbm, f32[1,512]{1,0:T(1,128)} %bitcast.5), custom_call_target="tpu_custom_call" | custom-call | tf_op jit(solution)/shard_map/spod/pallas_call | solution.py:462
  64.6 0.7 hand_over.1

commit v8 on v6

--- a/solution.py
+++ b/solution.py
@@ -1,3 +1,4 @@
+import functools
 import math
 
 import jax
@@ -80,7 +81,7 @@
     unit = unit_of(sx, y, c)
 
     loads = [
-        pltpu.make_async_copy(x_hbm.at[:, pl.ds(q * 128, 128)], xin.at[q], in_sem.at[q])
+        pltpu.make_async_copy(x_hbm.at[:, :, pl.ds(q * 128, 128)], xin.at[q], in_sem.at[q])
         for q in range(4)
     ]
     for load in loads:
@@ -122,16 +123,21 @@
         window = cosine * cosine * (1.0 / math.sqrt(0.375 * NT))
         factor.append([window * root_w[:, 128 * q : 128 * q + 128] for q in range(4)])
 
-    @pl.loop(0, 32)
-    def _(b):
-        owner = b >> 2
-        base = (owner >> 1) * 16 + (owner & 1)
+    def arrange(half, bt):
+        rows = pl.ds(pl.multiple_of(bt * 8, 8), 8)
+        base = bt * 16
         for q in range(4):
-            t0 = xin[q, pl.ds(b, 8, stride=32), :] * factor[0][q]
-            t1 = xin[q, pl.ds(256 + b, 8, stride=32), :] * factor[1][q]
-            even, odd = interleave(t0, t1, low)
-            sb[base + 4 * q, b & 3] = even
-            sb[base + 4 * q + 2, b & 3] = odd
+            early = jnp.swapaxes(xin[q, 0:8, rows, :], 0, 1)
+            late = jnp.swapaxes(xin[q, 8:16, rows, :], 0, 1)
+            for n in (0, 1, 4, 5):
+                b = n + 2 * half
+                even, odd = interleave(
+                    early[b] * factor[0][q], late[b] * factor[1][q], low
+                )
+                sb[base + n // 4 + 4 * q, b % 4] = even
+                sb[base + n // 4 + 4 * q + 2, b % 4] = odd
+
+    pl.loop(0, 4)(functools.partial(arrange, 0))
 
     groups = (pl.ds(0, 2), pl.ds(2, 1), pl.ds(3, 1))
 
@@ -160,6 +166,7 @@
     def _(k):
         send_columns(0, target(k))
 
+    pl.loop(0, 4)(functools.partial(arrange, 1))
     pl.semaphore_wait(step_sem, 3)
 
     @pl.loop(16, 64)
@@ -189,7 +196,8 @@
                 eh[parity, pl.ds(i * 64, 64), :] = early.astype(BF16)
                 eh[parity, pl.ds(256 + i * 64, 64), :] = late.astype(BF16)
 
-        here = pl.ds(pl.multiple_of((sx * 32 + 4 * p + h) * 16, 16), 16)
+        here = pl.ds(pl.multiple_of((sx * 32 + 4 * p + h) * 16 + 8, 8), 16)
+        turn = 4 * (p & 1) + h
 
         @pl.loop(0, 2)
         def _(step):
@@ -199,9 +207,9 @@
             total = product[0:512] + product[512:1024]
             total = total + pltpu.roll(total, 64, 1)
             for n in range(16):
-                ob[h, parity * 16 + n] = jnp.where(
-                    low16, total[32 * n : 32 * n + 16], total[32 * n + 16 : 32 * n + 32]
-                )
+                for m in (32 * n, 32 * n + 8):
+                    tile = jnp.where(low, total[m : m + 8], total[m + 16 : m + 24])
+                    ob[h, parity * 16 + n, m % 32 : m % 32 + 8, :] = pltpu.roll(tile, turn, 0)
 
             @pl.loop(0, 16 - step)
             def _(k):
@@ -220,6 +228,16 @@
 
     low32 = lax.broadcasted_iota(jnp.int32, (32, 128), 1) < 64
 
+    def slot_rows(x, j):
+        wrapped = row + (j & 7) >= 8
+        tiles = []
+        for g in range(4):
+            start = 8 + x * 512 + g * 128 + j
+            plain = db[pl.ds(start, 8, stride=17), :]
+            back = db[pl.ds(start - 8, 8, stride=17), :]
+            tiles.append(jnp.where(wrapped, back, plain))
+        return jnp.concatenate(tiles, axis=0)
+
     @pl.loop(0, 8)
     def _(i):
         zt = far_first(z, i)
@@ -229,8 +247,8 @@
             keep = jnp.where((unit == 0) & (j == 0), 0.0, 1.0).astype(F32)
             real, imag = [], []
             for x in range(0, NX, 2):
-                first = db[pl.ds(x * 512 + j, 32, stride=16), :]
-                second = db[pl.ds(x * 512 + 512 + j, 32, stride=16), :]
+                first = slot_rows(x, j)
+                second = slot_rows(x + 1, j)
                 r, m = interleave(first, second, low32)
                 real.append(r)
                 imag.append(m)
@@ -460,14 +478,14 @@
         in_specs=[any_spec, any_spec, any_spec],
         out_specs=(vmem, vmem),
         scratch_shapes=[
-            pltpu.VMEM((4, 512, 128), F32),
+            pltpu.VMEM((4, 16, 32, 128), F32),
             pltpu.VMEM((1, 512), F32),
             pltpu.VMEM((2, 1024, 512), BF16),
             pltpu.VMEM((64, 4, 8, 128), F32),
             pltpu.VMEM((64, 4, 8, 128), F32),
             pltpu.VMEM((2, 512, 128), BF16),
             pltpu.VMEM((4, 32, 16, 128), F32),
-            pltpu.VMEM((2048, 128), F32),
+            pltpu.VMEM((2064, 128), F32),
             pltpu.VMEM((512, 512), BF16),
             pltpu.VMEM((512, 512), BF16),
             pltpu.VMEM((8, 32, 128), F32),
@@ -483,7 +501,7 @@
         ],
         compiler_params=pltpu.CompilerParams(collective_id=0, has_side_effects=True),
         name="spod",
-    )(snapshots.reshape(times * blocks, points), table, weights)
+    )(snapshots, table, weights)
     modes, energies = pl.pallas_call(
         hand_over,
         out_shape=(

time: 66.5 us -> 65.5 us (0.985)
  Pallas kernels: 65.8 us -> 64.8 us
    pallas_call x1, Pallas kernels: 65.2 us -> 64.1 us  [body(): pl.pallas_call(kernel, out_shape=(pltpu.VMEM((32, 512), F32), pltpu.VMEM(...]
where the time goes in v8:
time: 65.5 us; the launch traced here: 65.4 us
  Pallas kernels  64.8 us (99%)
    pallas_call x1, Pallas kernels, body(): pl.pallas_call(kernel, out_shape=(pltpu.VMEM((32, 512), F32), pltpu.VMEM(...  64.1 us

profile of v8, /device:TPU:1, one launch (start us, length us, event | category | flops | bytes accessed | tf_op | source)
XLA Modules:
  0.0 65.4 jit_solution(11794682073584270891)
XLA Ops:
  0.6 64.1 %spod.1 = (f32[32,512]{1,0:T(8,128)S(1)}, f32[1,16]{1,0:T(1,128)S(1)}) custom-call(f32[16,32,512]{2,1,0:T(8,128)} %x_hbm.1, bf16[2,1024,512]{2,1,0:T(8,128)(2,1)} %constant.2.clone.tab_hbm, f32[1,512]{1,0:T(1,128)} %bitcast.3), custom_call_target="tpu_custom_call" | custom-call | tf_op jit(solution)/shard_map/spod/pallas_call | solution.py:475
  64.8 0.7 hand_over.1

commit v9 on v8

--- a/solution.py
+++ b/solution.py
@@ -171,7 +171,7 @@
 
     @pl.loop(16, 64)
     def _(k):
-        send_columns(0, target(k))
+        send_columns(0, target(79 - k))
 
     send_rest(1)
     send_rest(2)

time: 65.5 us -> 65.1 us (level)
  no operation moved by 1% of the time
where the time goes in v9:
time: 65.1 us; the launch traced here: 65 us
  Pallas kernels  64.3 us (99%)
    pallas_call x1, Pallas kernels, body(): pl.pallas_call(kernel, out_shape=(pltpu.VMEM((32, 512), F32), pltpu.VMEM(...  63.7 us

profile of v9, /device:TPU:1, one launch (start us, length us, event | category | flops | bytes accessed | tf_op | source)
XLA Modules:
  0.0 65.0 jit_solution(11097435604476355999)
XLA Ops:
  0.6 63.7 %spod.1 = (f32[32,512]{1,0:T(8,128)S(1)}, f32[1,16]{1,0:T(1,128)S(1)}) custom-call(f32[16,32,512]{2,1,0:T(8,128)} %x_hbm.1, bf16[2,1024,512]{2,1,0:T(8,128)(2,1)} %constant.2.clone.tab_hbm, f32[1,512]{1,0:T(1,128)} %bitcast.3), custom_call_target="tpu_custom_call" | custom-call | tf_op jit(solution)/shard_map/spod/pallas_call | solution.py:475
  64.3 0.7 %hand_over.1 = (f32[32,512]{1,0:T(8,128)}, f32[1,16]{1,0:T(1,128)}) custom-call(f32[32,512]{1,0:T(8,128)S(1)} %get-tuple-element.6.modes_ref, f32[1,16]{1,0:T(1,128)S(1)} %get-tuple-element.7.e_ref), custom_call_target="tpu_custom_call" | custom-call | tf_op jit(solution)/shard_map/hand_over/pallas_call | solution.py:505

commit v10 on v9

--- a/solution.py
+++ b/solution.py
@@ -156,7 +156,7 @@
     def send_rest(group):
         @pl.loop(1, 64)
         def _(k):
-            send_columns(group, target(64 - k))
+            send_columns(group, target((64 - k) ^ jnp.where(64 - k >= 32, 16, 0)))
 
     pl.semaphore_wait(barrier, 15 + 3 + 3)
     for k in range(1, 4):

time: 65.1 us -> 64.9 us (level)
  no operation moved by 1% of the time
where the time goes in v10:
time: 64.9 us
  Pallas kernels  64.2 us (99%)
    pallas_call x1, Pallas kernels, body(): pl.pallas_call(kernel, out_shape=(pltpu.VMEM((32, 512), F32), pltpu.VMEM(...  63.6 us

profile of v10, /device:TPU:1, one launch (start us, length us, event | category | flops | bytes accessed | tf_op | source)
XLA Modules:
  0.0 64.9 jit_solution(9306581351729539614)
XLA Ops:
  0.6 63.6 %spod.1 = (f32[32,512]{1,0:T(8,128)S(1)}, f32[1,16]{1,0:T(1,128)S(1)}) custom-call(f32[16,32,512]{2,1,0:T(8,128)} %x_hbm.1, bf16[2,1024,512]{2,1,0:T(8,128)(2,1)} %constant.2.clone.tab_hbm, f32[1,512]{1,0:T(1,128)} %bitcast.3), custom_call_target="tpu_custom_call" | custom-call | tf_op jit(solution)/shard_map/spod/pallas_call | solution.py:475
  64.2 0.7 %hand_over.1 = (f32[32,512]{1,0:T(8,128)}, f32[1,16]{1,0:T(1,128)}) custom-call(f32[32,512]{1,0:T(8,128)S(1)} %get-tuple-element.6.modes_ref, f32[1,16]{1,0:T(1,128)S(1)} %get-tuple-element.7.e_ref), custom_call_target="tpu_custom_call" | custom-call | tf_op jit(solution)/shard_map/hand_over/pallas_call | solution.py:505
